TPU v7x, 128 devices: a whole 4x4x4 slice. The times are simulated.
128 devices in a mesh: src: 8 (over z_hi, y), obs: 16 (over x, z_lo, core).
Axes of the slice: x: 4, y: 4, z: 4 (z_hi: 2, z_lo: 2; z = z_hi * 2 + z_lo), core: 2. Of those that a mesh axis runs over, the one named last changes fastest.
Arguments:
- tiles: bfloat16 [8, 16, 512, 128, 128], P('src', 'obs'), may hold values from -0.25 to 0.25
- tile_index: int32 [8, 16, 3, 512], P('src', 'obs'), may hold values from 0 to 1023, as said below
- tile_count: int32 [8, 16], P('src', 'obs'), may hold values from 64 to 512, as said below
- history: bfloat16 [16, 4, 1048576], P(None, None, ('src', 'obs')), may hold values from -6 to 6
- incident: float32 [2, 4, 1048576], P(None, None, ('src', 'obs')), may hold values from -6 to 6
- near_inverse: bfloat16 [8192, 128, 128], P(('src', 'obs')), may hold values from -0.5 to 0.5
Outputs:
- densities: bfloat16 [2, 4, 1048576], P(None, None, ('src', 'obs'))
Inputs may be any that keep to these rules, and one draw needn't show every extreme that they name: `tile_index`: row 0 is an observer block among the 512 of a device, row 1 a source block among its 1024, row 2 a delay slot below 16; slots at or past the device's count are padding; a tile may repeat. `tile_count`: live tile slots of each device, the first ones of its list.
All inputs are finite; a program needn't handle non-finite values.
Results may differ from a plain program's by a relative error of at most 0.005.
Values may be sent and summed in bfloat16 or wider, within the bound.
A program may use at most 128 MiB of HBM per device.

v0:
```python
import jax
import jax.numpy as jnp
from jax import lax
from jax.sharding import PartitionSpec as P


def on_device(tiles, tile_index, tile_count, history, incident, near_inverse):
    tile_rows = tiles.reshape(tiles.shape[2], tiles.shape[3], tiles.shape[4])
    index_rows = tile_index.reshape(3, tile_index.shape[3])
    live_count = tile_count.reshape(())
    blocks_own = near_inverse.shape[0]
    tile_width = near_inverse.shape[1]
    coefficients = history.shape[1]
    slot_count = history.shape[0]
    observer_owned = blocks_own * lax.axis_size("src")
    total_tiles = tile_rows.shape[0]
    group_size = min(64, total_tiles)
    loop_turns = total_tiles // group_size

    def accumulate(chooser):

        def one_group(turn_index, partial_value):
            start = turn_index * group_size
            tile_part = lax.dynamic_slice_in_dim(tile_rows, start, group_size, 0)
            index_part = lax.dynamic_slice_in_dim(index_rows, start, group_size, 1)
            operand = chooser(index_part, start)
            products = jnp.einsum(
                "gck,gki->cgi", operand, tile_part, preferred_element_type=jnp.float32
            )
            alive_mask = start + jnp.arange(group_size, dtype=jnp.int32) < live_count
            products = jnp.where(alive_mask[None, :, None], products, 0.0)
            return partial_value.at[:, index_part[0]].add(products)

        initial = jnp.zeros((coefficients, observer_owned, tile_width), jnp.float32)
        return lax.fori_loop(0, loop_turns, one_group, initial)

    def settle(partial_value, drive):
        summed = lax.psum(partial_value, "src")
        own_share = lax.dynamic_slice_in_dim(
            summed, lax.axis_index("src") * blocks_own, blocks_own, 1
        )
        right_side = (drive - own_share.reshape(coefficients, blocks_own * tile_width)).astype(
            jnp.bfloat16
        )
        right_side = right_side.reshape(coefficients, blocks_own, tile_width)
        solved = jnp.einsum(
            "cbk,bki->cbi", right_side, near_inverse, preferred_element_type=jnp.float32
        )
        return solved.reshape(coefficients, blocks_own * tile_width).astype(jnp.bfloat16)

    gathered = lax.all_gather(history, "obs", axis=2, tiled=True)
    history_src = gathered.reshape(slot_count, coefficients, -1, tile_width)

    def chooser_first(index_part, start):
        return history_src[index_part[2], :, index_part[1]]

    first_new = settle(accumulate(chooser_first), incident[0])
    newest_src = lax.all_gather(first_new, "obs", axis=1, tiled=True).reshape(
        coefficients, -1, tile_width
    )

    def chooser_second(index_part, start):
        source = index_part[1]
        delay_slot = index_part[2]
        older = history_src[jnp.maximum(delay_slot - 1, 0), :, source]
        newer = jnp.swapaxes(newest_src[:, source], 0, 1)
        return jnp.where((delay_slot == 0)[:, None, None], newer, older)

    second_new = settle(accumulate(chooser_second), incident[1])
    return jnp.stack([first_new, second_new])


def solution(mesh):
    in_specs = (
        P("src", "obs", None, None, None),
        P("src", "obs", None, None),
        P("src", "obs"),
        P(None, None, ("src", "obs")),
        P(None, None, ("src", "obs")),
        P(("src", "obs"), None, None),
    )
    out_specs = P(None, None, ("src", "obs"))
    return jax.shard_map(
        on_device, mesh=mesh, in_specs=in_specs, out_specs=out_specs, check_vma=False
    )
```

profile of v0, /device:TPU:1, one launch (start us, length us, event | category | flops | bytes accessed | tf_op | source)
XLA Modules:
  0.0 531.3 jit_solution(3474233912254696265)
XLA Ops:
  8.0 96.2 %all-gather.3.cloned.1.call-done = bf16[16,4,131072]{2,1,0:T(4,128)(2,1)} async-done(((bf16[16,4,8192]{2,1,0:T(4,128)(2,1)}), bf16[16,4,131072]{2,1,0:T(4,128)(2,1)}) %all-gather.3.cloned.1.call-update) | async-done | bytes 16777232 | tf_op jit(solution)/shard_map/all_gather | solution.py:51
  104.4 98.3 %while.28 = (s32[]{:T(128)}, f32[4,512,128]{2,0,1:T(4,128)S(1)}, s32[3,512]{1,0:T(4,128)S(1)}, s32[]{:T(128)}, bf16[512,128,128]{2,1,0:T(8,128)(2,1)}, /*index=5...) while((s32[]{:T(128)}, f32[4,512,128]{2,0,1:T(4,128)S(1)}, ...), condition=%wide.region_2.3_spmd, body=%wide.region_0.2_spmd.sunk | while | flops 8455174 | bytes 2821923 | solution.py:35
  105.1 6.5 %gather_fusion = bf16[64,4,128]{2,1,0:T(4,128)(2,1)S(1)} fusion(bf16[16,4,1024,128]{3,1,2,0:T(4,128)(2,1)} %get-tuple-element.438, s32[64]{0:T(128)S(1)} %get-tuple-element.402), kind=kCustom, calls=%fused_computation.clone.1 | custom fusion | bytes 131584 | tf_op jit(solution)/shard_map/while/body/eval_jaxpr/gather | solution.py:55
  113.9 2.7 scatter_fusion
  117.4 6.5 %gather_fusion = bf16[64,4,128]{2,1,0:T(4,128)(2,1)S(1)} fusion(bf16[16,4,1024,128]{3,1,2,0:T(4,128)(2,1)} %get-tuple-element.438, s32[64]{0:T(128)S(1)} %get-tuple-element.402), kind=kCustom, calls=%fused_computation.clone.1 | custom fusion | bytes 131584 | tf_op jit(solution)/shard_map/while/body/eval_jaxpr/gather | solution.py:55
  126.2 2.7 scatter_fusion
  129.7 6.5 %gather_fusion = bf16[64,4,128]{2,1,0:T(4,128)(2,1)S(1)} fusion(bf16[16,4,1024,128]{3,1,2,0:T(4,128)(2,1)} %get-tuple-element.438, s32[64]{0:T(128)S(1)} %get-tuple-element.402), kind=kCustom, calls=%fused_computation.clone.1 | custom fusion | bytes 131584 | tf_op jit(solution)/shard_map/while/body/eval_jaxpr/gather | solution.py:55
  138.5 2.7 scatter_fusion
  142.0 6.5 %gather_fusion = bf16[64,4,128]{2,1,0:T(4,128)(2,1)S(1)} fusion(bf16[16,4,1024,128]{3,1,2,0:T(4,128)(2,1)} %get-tuple-element.438, s32[64]{0:T(128)S(1)} %get-tuple-element.402), kind=kCustom, calls=%fused_computation.clone.1 | custom fusion | bytes 131584 | tf_op jit(solution)/shard_map/while/body/eval_jaxpr/gather | solution.py:55
  150.8 2.8 scatter_fusion
  154.3 6.5 %gather_fusion = bf16[64,4,128]{2,1,0:T(4,128)(2,1)S(1)} fusion(bf16[16,4,1024,128]{3,1,2,0:T(4,128)(2,1)} %get-tuple-element.438, s32[64]{0:T(128)S(1)} %get-tuple-element.402), kind=kCustom, calls=%fused_computation.clone.1 | custom fusion | bytes 131584 | tf_op jit(solution)/shard_map/while/body/eval_jaxpr/gather | solution.py:55
  163.1 2.7 scatter_fusion
  166.6 6.5 %gather_fusion = bf16[64,4,128]{2,1,0:T(4,128)(2,1)S(1)} fusion(bf16[16,4,1024,128]{3,1,2,0:T(4,128)(2,1)} %get-tuple-element.438, s32[64]{0:T(128)S(1)} %get-tuple-element.402), kind=kCustom, calls=%fused_computation.clone.1 | custom fusion | bytes 131584 | tf_op jit(solution)/shard_map/while/body/eval_jaxpr/gather | solution.py:55
  175.4 2.7 scatter_fusion
  178.9 6.5 %gather_fusion = bf16[64,4,128]{2,1,0:T(4,128)(2,1)S(1)} fusion(bf16[16,4,1024,128]{3,1,2,0:T(4,128)(2,1)} %get-tuple-element.438, s32[64]{0:T(128)S(1)} %get-tuple-element.402), kind=kCustom, calls=%fused_computation.clone.1 | custom fusion | bytes 131584 | tf_op jit(solution)/shard_map/while/body/eval_jaxpr/gather | solution.py:55
  187.7 2.7 scatter_fusion
  191.2 6.5 %gather_fusion = bf16[64,4,128]{2,1,0:T(4,128)(2,1)S(1)} fusion(bf16[16,4,1024,128]{3,1,2,0:T(4,128)(2,1)} %get-tuple-element.438, s32[64]{0:T(128)S(1)} %get-tuple-element.402), kind=kCustom, calls=%fused_computation.clone.1 | custom fusion | bytes 131584 | tf_op jit(solution)/shard_map/while/body/eval_jaxpr/gather | solution.py:55
  200.0 2.7 scatter_fusion
  203.8 82.6 %all-reduce.3.cloned.1.call-done = f32[4,512,128]{2,0,1:T(4,128)} async-done(((f32[4,512,128]{2,0,1:T(4,128)}), f32[4,512,128]{2,0,1:T(4,128)}) %all-reduce.3.cloned.1.call-update) | async-done | bytes 1048592 | tf_op jit(solution)/shard_map/psum | solution.py:38
  288.8 36.3 %all-gather.5.cloned.1.call-done = bf16[4,131072]{1,0:T(4,128)(2,1)} async-done(((bf16[4,8192]{1,0:T(4,128)(2,1)}), bf16[4,131072]{1,0:T(4,128)(2,1)}) %all-gather.5.cloned.1.call-update) | async-done | bytes 1048592 | tf_op jit(solution)/shard_map/all_gather | solution.py:58
  325.3 114.0 %while.29 = (s32[]{:T(128)}, f32[4,512,128]{2,0,1:T(4,128)S(1)}, s32[3,512]{1,0:T(4,128)S(1)}, s32[]{:T(128)}, bf16[512,128,128]{2,1,0:T(8,128)(2,1)}, /*index=5...) while((s32[]{:T(128)}, f32[4,512,128]{2,0,1:T(4,128)S(1)}, ...), condition=%wide.region_6.7_spmd, body=%wide.region_4.6_spmd.sunk | while | flops 8488966 | bytes 3023787 | solution.py:35
  327.9 6.5 %gather_fusion.2 = bf16[64,4,128]{2,1,0:T(4,128)(2,1)S(1)} fusion(bf16[16,4,1024,128]{3,1,2,0:T(4,128)(2,1)} %get-tuple-element.471, s32[64]{0:T(128)S(1)} %get-tuple-element.412), kind=kCustom, calls=%fused_computation.2.clone.1 | custom fusion | bytes 131584 | tf_op jit(solution)/shard_map/while/body/eval_jaxpr/gather | solution.py:65
  342.2 6.5 %gather_fusion.2 = bf16[64,4,128]{2,1,0:T(4,128)(2,1)S(1)} fusion(bf16[16,4,1024,128]{3,1,2,0:T(4,128)(2,1)} %get-tuple-element.471, s32[64]{0:T(128)S(1)} %get-tuple-element.412), kind=kCustom, calls=%fused_computation.2.clone.1 | custom fusion | bytes 131584 | tf_op jit(solution)/shard_map/while/body/eval_jaxpr/gather | solution.py:65
  356.4 6.5 %gather_fusion.2 = bf16[64,4,128]{2,1,0:T(4,128)(2,1)S(1)} fusion(bf16[16,4,1024,128]{3,1,2,0:T(4,128)(2,1)} %get-tuple-element.471, s32[64]{0:T(128)S(1)} %get-tuple-element.412), kind=kCustom, calls=%fused_computation.2.clone.1 | custom fusion | bytes 131584 | tf_op jit(solution)/shard_map/while/body/eval_jaxpr/gather | solution.py:65
  370.7 6.5 %gather_fusion.2 = bf16[64,4,128]{2,1,0:T(4,128)(2,1)S(1)} fusion(bf16[16,4,1024,128]{3,1,2,0:T(4,128)(2,1)} %get-tuple-element.471, s32[64]{0:T(128)S(1)} %get-tuple-element.412), kind=kCustom, calls=%fused_computation.2.clone.1 | custom fusion | bytes 131584 | tf_op jit(solution)/shard_map/while/body/eval_jaxpr/gather | solution.py:65
  379.5 2.7 scatter_fusion.1
  385.0 6.5 %gather_fusion.2 = bf16[64,4,128]{2,1,0:T(4,128)(2,1)S(1)} fusion(bf16[16,4,1024,128]{3,1,2,0:T(4,128)(2,1)} %get-tuple-element.471, s32[64]{0:T(128)S(1)} %get-tuple-element.412), kind=kCustom, calls=%fused_computation.2.clone.1 | custom fusion | bytes 131584 | tf_op jit(solution)/shard_map/while/body/eval_jaxpr/gather | solution.py:65
  399.2 6.5 %gather_fusion.2 = bf16[64,4,128]{2,1,0:T(4,128)(2,1)S(1)} fusion(bf16[16,4,1024,128]{3,1,2,0:T(4,128)(2,1)} %get-tuple-element.471, s32[64]{0:T(128)S(1)} %get-tuple-element.412), kind=kCustom, calls=%fused_computation.2.clone.1 | custom fusion | bytes 131584 | tf_op jit(solution)/shard_map/while/body/eval_jaxpr/gather | solution.py:65
  413.5 6.5 %gather_fusion.2 = bf16[64,4,128]{2,1,0:T(4,128)(2,1)S(1)} fusion(bf16[16,4,1024,128]{3,1,2,0:T(4,128)(2,1)} %get-tuple-element.471, s32[64]{0:T(128)S(1)} %get-tuple-element.412), kind=kCustom, calls=%fused_computation.2.clone.1 | custom fusion | bytes 131584 | tf_op jit(solution)/shard_map/while/body/eval_jaxpr/gather | solution.py:65
  427.7 6.5 %gather_fusion.2 = bf16[64,4,128]{2,1,0:T(4,128)(2,1)S(1)} fusion(bf16[16,4,1024,128]{3,1,2,0:T(4,128)(2,1)} %get-tuple-element.471, s32[64]{0:T(128)S(1)} %get-tuple-element.412), kind=kCustom, calls=%fused_computation.2.clone.1 | custom fusion | bytes 131584 | tf_op jit(solution)/shard_map/while/body/eval_jaxpr/gather | solution.py:65
  436.5 2.7 scatter_fusion.1
  440.3 82.0 %all-reduce.5.cloned.1.call-done = f32[4,512,128]{2,0,1:T(4,128)} async-done(((f32[4,512,128]{2,0,1:T(4,128)}), f32[4,512,128]{2,0,1:T(4,128)}) %all-reduce.5.cloned.1.call-update) | async-done | bytes 1048592 | tf_op jit(solution)/shard_map/psum | solution.py:38
  (116 shorter events, 88.3 us)
Async XLA Ops:
  6.5 279.9 %copy-start = (bf16[64,128,128]{2,1,0:T(8,128)(2,1)S(1)}, bf16[64,128,128]{2,1,0:T(8,128)(2,1)}, u32[]{:S(2)}) copy-start(bf16[64,128,128]{2,1,0:T(8,128)(2,1)} %param.15) | copy-start | bytes 6291460
  6.5 97.7 %all-gather.3.cloned.1.call-start = ((), (), s32[]{:S(2)}) async-start(), calls=%async_computation | async-start | bytes 17825792 | tf_op jit(solution)/shard_map/all_gather | solution.py:51
  7.3 279.2 %all-reduce.3.cloned.1.call-start = ((), (), s32[]{:S(2)}) async-start(), calls=%async_computation.1 | async-start | bytes 2097152 | tf_op jit(solution)/shard_map/psum | solution.py:38
  202.7 1.0 copy-start.2
  203.8 121.3 %all-gather.5.cloned.1.call-start = ((), (), s32[]{:S(2)}) async-start(), calls=%async_computation.2 | async-start | bytes 1114112 | tf_op jit(solution)/shard_map/all_gather | solution.py:58
  288.7 233.6 %all-reduce.5.cloned.1.call-start = ((), (), s32[]{:S(2)}) async-start(), calls=%async_computation.3 | async-start | bytes 2097152 | tf_op jit(solution)/shard_map/psum | solution.py:38
  439.3 1.0 copy-start.1
  439.3 84.7 %copy-start.3 = (bf16[64,4,128]{2,1,0:T(4,128)(2,1)S(1)}, bf16[64,4,128]{2,1,0:T(4,128)(2,1)}, u32[]{:S(2)}) copy-start(bf16[64,4,128]{2,1,0:T(4,128)(2,1)} %convolution_convert_fusion.1) | copy-start | bytes 196612
Sparse Core Ops, SparseCore 0:
  9.0 95.1 all-gather.2
  203.9 82.5 all-reduce.2
  288.9 36.2 all-gather.4
  440.5 81.8 all-reduce.4
where the time goes:
time: 538 us; the launch traced here: 531 us
  waiting for transfers between devices  298 us (55%)
  local copies, waits for them, and re-layouts  124 us (23%)
  other arithmetic  55.4 us (10%)
  matrix products  40.1 us (7%)
  between operations  13.2 us (2%)
    psum x2, waiting for transfers between devices, settle(): summed = lax.psum(partial_value, 'src')  165 us
    all_gather x1, waiting for transfers between devices, on_device(): gathered = lax.all_gather(history, 'obs', axis=2, tiled=True)  96.2 us
    gather x8, local copies, waits for them, and re-layouts, chooser_second(): older = history_src[jnp.maximum(delay_slot - 1, 0), :, source]  52.3 us
    gather x8, local copies, waits for them, and re-layouts, chooser_first(): return history_src[index_part[2], :, index_part[1]]  52.2 us
    scatter-add x16, other arithmetic, one_group(): return partial_value.at[:, index_part[0]].add(products)  43.9 us
    all_gather x1, waiting for transfers between devices, on_device(): lax.all_gather(first_new, 'obs', axis=1, tiled=True)  36.3 us
    dot_general x16, matrix products, one_group(): jnp.einsum('gck,gki->cgi', operand, tile_part, preferred_element_type=jnp...  36.3 us
    gather x8, local copies, waits for them, and re-layouts, chooser_second(): newer = jnp.swapaxes(newest_src[:, source], 0, 1)  15 us
  transfers between devices with their start and end apart: 4, of which 4 were waited for; matrix products, arithmetic and copies ran while one was open for 0% of the time, Pallas kernels for 0%

commit v1 on v0

v1 whole, which is shorter than its diff:
```python
import functools

import jax
import jax.numpy as jnp
from jax import lax
from jax.experimental import pallas as pl
from jax.experimental.pallas import tpu as pltpu
from jax.sharding import PartitionSpec as P

MESH = pl.DeviceIdType.MESH
CAP = 64
CAP0 = 16
FAR = -(1 << 20)


def greet(src_peers, obs_peers, n_src, n_obs):
    me_s, me_o = lax.axis_index("src"), lax.axis_index("obs")
    barrier = pltpu.get_barrier_semaphore()
    if src_peers:
        for k in range(1, n_src):
            pl.semaphore_signal(
                barrier, inc=1, device_id=(lax.rem(me_s + k, n_src), me_o), device_id_type=MESH
            )
    if obs_peers:
        for k in range(1, n_obs):
            pl.semaphore_signal(
                barrier, inc=1, device_id=(me_s, lax.rem(me_o + k, n_obs)), device_id_type=MESH
            )
    total = (n_src - 1) * src_peers + (n_obs - 1) * obs_peers
    return lambda: pl.semaphore_wait(barrier, total)


def to_obs(k, n_obs, src_ref, dst_ref, send_sem, recv_sem):
    me_s, me_o = lax.axis_index("src"), lax.axis_index("obs")
    return pltpu.make_async_remote_copy(
        src_ref=src_ref, dst_ref=dst_ref, send_sem=send_sem.at[k], recv_sem=recv_sem.at[k],
        device_id=(me_s, lax.rem(me_o + k, n_obs)), device_id_type=MESH,
    )


def to_src(k, n_src, src_ref, dst_ref, send_sem, recv_sem):
    me_s, me_o = lax.axis_index("src"), lax.axis_index("obs")
    return pltpu.make_async_remote_copy(
        src_ref=src_ref, dst_ref=dst_ref, send_sem=send_sem.at[k], recv_sem=recv_sem.at[k],
        device_id=(lax.rem(me_s + k, n_src), me_o), device_id_type=MESH,
    )


def request_kernel(n_src, n_obs, bd, idx_ref, cnt_ref, recv_ref, info_ref, send_ref, send_sem, recv_sem):
    me = lax.axis_index("obs")
    entered = greet(0, 1, n_src, n_obs)
    n_tiles = idx_ref.shape[1]
    shift = bd.bit_length() - 1
    lane = lax.broadcasted_iota(jnp.int32, (1, n_tiles), 1)
    live = lane < cnt_ref[0, 0]
    obs_block = idx_ref[0:1, :]
    source = idx_ref[1:2, :]
    delay = idx_ref[2:3, :]
    owner = lax.shift_right_logical(source, shift)
    place = jnp.bitwise_and(source, bd - 1)
    owner_row = lax.broadcasted_iota(jnp.int32, (n_obs, n_tiles), 0)
    mine = jnp.where(jnp.logical_and(owner == owner_row, live), 1.0, 0.0)
    mine0 = jnp.where(delay == 0, mine, 0.0)
    before = jnp.where(
        lax.broadcasted_iota(jnp.int32, (n_tiles, n_tiles), 0)
        < lax.broadcasted_iota(jnp.int32, (n_tiles, n_tiles), 1),
        1.0, 0.0,
    ).astype(jnp.bfloat16)
    order = jnp.dot(mine.astype(jnp.bfloat16), before, preferred_element_type=jnp.float32)
    order0 = jnp.dot(mine0.astype(jnp.bfloat16), before, preferred_element_type=jnp.float32)
    rank = jnp.sum(order * mine, axis=0, keepdims=True)
    rank0 = jnp.sum(order0 * mine0, axis=0, keepdims=True)
    newest = jnp.logical_and(live, delay == 0)
    over = jnp.where(live, jnp.where(rank >= CAP, 1.0, 0.0), 0.0) + jnp.where(
        newest, jnp.where(rank0 >= CAP0, 1.0, 0.0), 0.0
    )
    flag = jnp.max(over, axis=1, keepdims=True)
    rank = rank.astype(jnp.int32)
    rank0 = rank0.astype(jnp.int32)
    fits = jnp.logical_and(live, rank < CAP)
    fits0 = jnp.logical_and(newest, rank0 < CAP0)
    slot = jnp.where(fits, owner * CAP + rank, 0)
    slot0 = jnp.where(fits0, n_obs * CAP + owner * CAP0 + rank0, 0)
    info_ref[0:1, :] = slot
    info_ref[1:2, :] = jnp.where(fits, obs_block, n_src * bd)
    info_ref[2:3, :] = jnp.where(newest, slot0, slot)
    info_ref[3:8, :] = jnp.zeros((5, n_tiles), jnp.int32)
    key = jnp.where(fits, owner * 128 + rank, FAR)
    key0 = jnp.where(fits0, owner * 128 + CAP + rank0, FAR)
    code_row = lax.broadcasted_iota(jnp.int32, (16, n_tiles), 0)
    codes = jnp.where(code_row == 0, place, jnp.where(code_row == 1, delay, 0))
    codes = codes.astype(jnp.float32).astype(jnp.bfloat16)
    row = lax.broadcasted_iota(jnp.int32, (128, n_tiles), 0)
    out_lane = lax.broadcasted_iota(jnp.int32, (1, 128), 1)

    def one_owner(o, carry):
        hit = jnp.logical_or(key - o * 128 == row, key0 - o * 128 == row)
        pick = jnp.where(hit, 1.0, 0.0).astype(jnp.bfloat16)
        found = lax.dot_general(
            codes, pick, (((1,), (1,)), ((), ())), preferred_element_type=jnp.float32
        )
        code = found[0:1, :] + found[1:2, :] * bd
        code = jnp.where(out_lane == 127, flag, code)
        send_ref[o] = code.astype(jnp.int32)
        return carry

    lax.fori_loop(0, n_obs, one_owner, 0)
    recv_ref[me] = send_ref[me]
    entered()
    copies = []
    for k in range(1, n_obs):
        copy = to_obs(k, n_obs, send_ref.at[lax.rem(me + k, n_obs)], recv_ref.at[me], send_sem, recv_sem)
        copy.start()
        copies.append(copy)
    for copy in copies:
        copy.wait()


def gather_rows(req_ref, table_ref, out_ref, dest, slots, first, code_to_row):
    step = 8

    def one(turn, carry):
        for i in range(step):
            r = turn * step + i
            out_ref[r] = table_ref[code_to_row(req_ref[dest, 0, first + r])]
        return carry

    lax.fori_loop(0, slots // step, one, 0)


def rows_kernel(n_src, n_obs, bd, req_ref, hist_ref, rows_ref, flags_ref, send, mark, own_sem, send_sem, recv_sem, fsend, frecv):
    me_s, me_o = lax.axis_index("src"), lax.axis_index("obs")
    entered = greet(1, 1, n_src, n_obs)
    flag = req_ref[0, 0, 127]
    for o in range(1, n_obs):
        flag = jnp.maximum(flag, req_ref[o, 0, 127])
    mark[...] = jnp.full(mark.shape, flag, jnp.int32)
    flags_ref[me_s] = mark[...]
    copies = []
    for k in range(1, n_obs):
        gather_rows(req_ref, hist_ref, send.at[k], lax.rem(me_o + k, n_obs), CAP, 0, lambda c: c)
        if k == 1:
            entered()
        copy = to_obs(k, n_obs, send.at[k], rows_ref.at[pl.ds(me_o * CAP, CAP)], send_sem, recv_sem)
        copy.start()
        copies.append(copy)
        if k == 1:
            for j in range(1, n_src):
                copy = to_src(j, n_src, mark, flags_ref.at[me_s], fsend, frecv)
                copy.start()
                copies.append(copy)
    gather_rows(req_ref, hist_ref, send.at[0], me_o, CAP, 0, lambda c: c)
    own = pltpu.make_async_copy(send.at[0], rows_ref.at[pl.ds(me_o * CAP, CAP)], own_sem)
    own.start()
    own.wait()
    for copy in copies:
        copy.wait()


def products_kernel(which, chunk, depth, info_ref, cnt_ref, tiles_ref, rows_ref, acc_ref, buf, sem):
    live = cnt_ref[0, 0]
    chunks = (live + chunk - 1) // chunk

    def fetch(c, slot):
        return pltpu.make_async_copy(tiles_ref.at[pl.ds(c * chunk, chunk)], buf.at[slot], sem.at[slot])

    for c in range(min(depth - 1, tiles_ref.shape[0] // chunk)):
        @pl.when(c < chunks)
        def _():
            fetch(c, c).start()

    acc_ref[...] = jnp.zeros_like(acc_ref)

    def one_chunk(c, carry):
        slot = lax.rem(c, depth)

        @pl.when(c + depth - 1 < chunks)
        def _():
            fetch(c + depth - 1, lax.rem(c + depth - 1, depth)).start()

        fetch(c, slot).wait()
        for i in range(chunk):
            t = c * chunk + i
            y = jnp.dot(rows_ref[info_ref[which, t]], buf[slot, i], preferred_element_type=jnp.float32)
            l = info_ref[1, t]
            acc_ref[l] = acc_ref[l] + y
        return carry

    lax.fori_loop(0, chunks, one_chunk, 0)


def scatter_start(n_src, bd, part_ref, recv, send_sem, recv_sem):
    me_s = lax.axis_index("src")
    copies = []
    for k in range(1, n_src):
        peer = lax.rem(me_s + k, n_src)
        copy = to_src(k, n_src, part_ref.at[pl.ds(peer * bd, bd)], recv.at[k], send_sem, recv_sem)
        copy.start()
        copies.append(copy)
    return copies


def reduce_solve(n_src, bd, part_ref, recv, inc_ref, near, new_ref):
    me_s = lax.axis_index("src")
    step = 8

    def one(turn, carry):
        at = pl.ds(turn * step, step)
        total = part_ref[pl.ds(me_s * bd + turn * step, step)]
        for k in range(1, n_src):
            total = total + recv[k, at]
        drive = (inc_ref[at] - total).astype(jnp.bfloat16)
        for i in range(step):
            b = turn * step + i
            new_ref[b] = jnp.dot(drive[i], near[b], preferred_element_type=jnp.float32).astype(jnp.bfloat16)
        return carry

    lax.fori_loop(0, bd // step, one, 0)


def first_kernel(
    n_src, n_obs, bd, req_ref, part_ref, inc_ref, near_ref, hist_ref, new_ref, rows_ref,
    recv, near, send, send0, near_sem, own_sem, rsend, rrecv, send_sem, recv_sem, send_sem0, recv_sem0,
):
    me_s, me_o = lax.axis_index("src"), lax.axis_index("obs")
    entered = greet(1, 1, n_src, n_obs)
    load = pltpu.make_async_copy(near_ref, near, near_sem)
    load.start()
    entered()
    reduce = scatter_start(n_src, bd, part_ref, recv, rsend, rrecv)
    older = lambda c: jnp.maximum(c - bd, 0)
    copies = []
    for k in range(1, n_obs):
        gather_rows(req_ref, hist_ref, send.at[k], lax.rem(me_o + k, n_obs), CAP, 0, older)
        copy = to_obs(k, n_obs, send.at[k], rows_ref.at[pl.ds(me_o * CAP, CAP)], send_sem, recv_sem)
        copy.start()
        copies.append(copy)
    gather_rows(req_ref, hist_ref, send.at[0], me_o, CAP, 0, older)
    own = pltpu.make_async_copy(send.at[0], rows_ref.at[pl.ds(me_o * CAP, CAP)], own_sem.at[0])
    own.start()
    load.wait()
    for copy in reduce:
        copy.wait()
    reduce_solve(n_src, bd, part_ref, recv, inc_ref, near, new_ref)
    base = n_obs * CAP
    place = lambda c: jnp.bitwise_and(c, bd - 1)
    for k in range(1, n_obs):
        gather_rows(req_ref, new_ref, send0.at[k], lax.rem(me_o + k, n_obs), CAP0, CAP, place)
        copy = to_obs(k, n_obs, send0.at[k], rows_ref.at[pl.ds(base + me_o * CAP0, CAP0)], send_sem0, recv_sem0)
        copy.start()
        copies.append(copy)
    gather_rows(req_ref, new_ref, send0.at[0], me_o, CAP0, CAP, place)
    own0 = pltpu.make_async_copy(send0.at[0], rows_ref.at[pl.ds(base + me_o * CAP0, CAP0)], own_sem.at[1])
    own0.start()
    own.wait()
    own0.wait()
    for copy in copies:
        copy.wait()


def second_kernel(n_src, n_obs, bd, part_ref, inc_ref, near_ref, new_ref, recv, near, near_sem, rsend, rrecv):
    entered = greet(1, 0, n_src, n_obs)
    load = pltpu.make_async_copy(near_ref, near, near_sem)
    load.start()
    entered()
    reduce = scatter_start(n_src, bd, part_ref, recv, rsend, rrecv)
    load.wait()
    for copy in reduce:
        copy.wait()
    reduce_solve(n_src, bd, part_ref, recv, inc_ref, near, new_ref)


def dense_path(tile_rows, index_rows, live_count, history, incident, near_inverse, n_src, n_obs):
    bd, width = near_inverse.shape[:2]
    slots, coefs = history.shape[:2]
    n_tiles = tile_rows.shape[0]
    group = min(64, n_tiles)

    def gather_obs(block):
        ring = [(i, (i + 1) % n_obs) for i in range(n_obs)]
        me = lax.axis_index("obs")
        whole = jnp.zeros((n_obs,) + block.shape, block.dtype)

        def hop(k, carry):
            whole, moving = carry
            whole = lax.dynamic_update_index_in_dim(whole, moving, lax.rem(me - k + n_obs, n_obs), 0)
            return whole, lax.ppermute(moving, "obs", ring)

        return lax.fori_loop(0, n_obs, hop, (whole, block))[0]

    def sum_src(value):
        ring = [(i, (i + 1) % n_src) for i in range(n_src)]

        def hop(k, carry):
            total, moving = carry
            moving = lax.ppermute(moving, "src", ring)
            return total + moving, moving

        return lax.fori_loop(0, n_src - 1, hop, (value, value))[0]

    def accumulate(chooser):
        def one_group(turn, partial):
            start = turn * group
            tile_part = lax.dynamic_slice_in_dim(tile_rows, start, group, 0)
            index_part = lax.dynamic_slice_in_dim(index_rows, start, group, 1)
            products = jnp.einsum(
                "gck,gki->gci", chooser(index_part), tile_part, preferred_element_type=jnp.float32
            )
            alive = start + jnp.arange(group, dtype=jnp.int32) < live_count
            products = jnp.where(alive[:, None, None], products, 0.0)
            return partial.at[index_part[0]].add(products)

        initial = jnp.zeros((bd * n_src, coefs, width), jnp.float32)
        return lax.fori_loop(0, n_tiles // group, one_group, initial)

    def settle(partial, drive):
        own = lax.dynamic_slice_in_dim(sum_src(partial), lax.axis_index("src") * bd, bd, 0)
        right = (drive - own).astype(jnp.bfloat16)
        solved = jnp.einsum("bck,bki->bci", right, near_inverse, preferred_element_type=jnp.float32)
        return solved.astype(jnp.bfloat16)

    past = gather_obs(history)

    def pick(block, index_part, slot):
        return past[index_part[1] // bd, slot, index_part[1] % bd]

    past = past.reshape(n_obs, slots, coefs, bd, width).transpose(0, 1, 3, 2, 4)
    first = settle(accumulate(lambda ip: pick(past, ip, ip[2])), incident[0])
    newest = gather_obs(first)

    def second_rows(ip):
        older = pick(past, ip, jnp.maximum(ip[2] - 1, 0))
        newer = newest[ip[1] // bd, ip[1] % bd]
        return jnp.where((ip[2] == 0)[:, None, None], newer, older)

    second = settle(accumulate(second_rows), incident[1])
    return jnp.stack([first, second])


def solution(mesh):
    n_src, n_obs = mesh.shape["src"], mesh.shape["obs"]
    vmem = pl.BlockSpec(memory_space=pltpu.VMEM)
    smem = pl.BlockSpec(memory_space=pltpu.SMEM)
    anywhere = pl.BlockSpec(memory_space=pl.ANY)
    dma = pltpu.SemaphoreType.DMA

    def params(i):
        return pltpu.CompilerParams(collective_id=i, has_side_effects=True)

    def on_device(tiles, tile_index, tile_count, history, incident, near_inverse):
        n_tiles, width = tiles.shape[2], tiles.shape[4]
        bd = near_inverse.shape[0]
        slots, coefs = history.shape[:2]
        tile_rows = tiles.reshape(n_tiles, width, width)
        index_rows = tile_index.reshape(3, n_tiles)
        hist = history.reshape(slots, coefs, bd, width).transpose(0, 2, 1, 3).reshape(slots * bd, coefs, width)
        drive = incident.reshape(2, coefs, bd, width).transpose(0, 2, 1, 3)
        row_slots = n_obs * CAP

        requests, info = pl.pallas_call(
            functools.partial(request_kernel, n_src, n_obs, bd),
            name="requests",
            out_shape=(
                jax.ShapeDtypeStruct((n_obs, 1, 128), jnp.int32),
                jax.ShapeDtypeStruct((8, n_tiles), jnp.int32),
            ),
            in_specs=[vmem, smem],
            out_specs=(vmem, vmem),
            scratch_shapes=[pltpu.VMEM((n_obs, 1, 128), jnp.int32), dma((n_obs,)), dma((n_obs,))],
            compiler_params=params(0),
        )(index_rows, tile_count)

        rows, flags = pl.pallas_call(
            functools.partial(rows_kernel, n_src, n_obs, bd),
            name="rows",
            out_shape=(
                jax.ShapeDtypeStruct((row_slots, coefs, width), jnp.bfloat16),
                jax.ShapeDtypeStruct((n_src, 1, 128), jnp.int32),
            ),
            in_specs=[smem, vmem],
            out_specs=(anywhere, vmem),
            scratch_shapes=[
                pltpu.VMEM((n_obs, CAP, coefs, width), jnp.bfloat16), pltpu.VMEM((1, 128), jnp.int32),
                dma, dma((n_obs,)), dma((n_obs,)), dma((n_src,)), dma((n_src,)),
            ],
            compiler_params=params(1),
        )(requests, hist)

        chunk, depth = min(32, n_tiles), 4

        def products(which, row_array):
            return pl.pallas_call(
                functools.partial(products_kernel, which, chunk, depth),
                name="products",
                out_shape=jax.ShapeDtypeStruct((n_src * bd + 8, coefs, width), jnp.float32),
                in_specs=[smem, smem, anywhere, vmem],
                out_specs=vmem,
                scratch_shapes=[pltpu.VMEM((depth, chunk, width, width), jnp.bfloat16), dma((depth,))],
            )(info, tile_count, tile_rows, row_array)

        part = products(0, rows)
        first, rows2 = pl.pallas_call(
            functools.partial(first_kernel, n_src, n_obs, bd),
            name="first",
            out_shape=(
                jax.ShapeDtypeStruct((bd, coefs, width), jnp.bfloat16),
                jax.ShapeDtypeStruct((row_slots + n_obs * CAP0, coefs, width), jnp.bfloat16),
            ),
            in_specs=[smem, vmem, vmem, anywhere, vmem],
            out_specs=(vmem, anywhere),
            scratch_shapes=[
                pltpu.VMEM((n_src, bd, coefs, width), jnp.float32),
                pltpu.VMEM((bd, width, width), jnp.bfloat16),
                pltpu.VMEM((n_obs, CAP, coefs, width), jnp.bfloat16),
                pltpu.VMEM((n_obs, CAP0, coefs, width), jnp.bfloat16),
                dma, dma((2,)), dma((n_src,)), dma((n_src,)),
                dma((n_obs,)), dma((n_obs,)), dma((n_obs,)), dma((n_obs,)),
            ],
            compiler_params=params(2),
        )(requests, part, drive[0], near_inverse, hist)
        part = products(2, rows2)
        second = pl.pallas_call(
            functools.partial(second_kernel, n_src, n_obs, bd),
            name="second",
            out_shape=jax.ShapeDtypeStruct((bd, coefs, width), jnp.bfloat16),
            in_specs=[vmem, vmem, anywhere],
            out_specs=vmem,
            scratch_shapes=[
                pltpu.VMEM((n_src, bd, coefs, width), jnp.float32),
                pltpu.VMEM((bd, width, width), jnp.bfloat16),
                dma, dma((n_src,)), dma((n_src,)),
            ],
            compiler_params=params(3),
        )(part, drive[1], near_inverse)
        both = jnp.stack([first, second])
        crowded = jnp.max(flags) > 0

        both = lax.cond(
            crowded,
            lambda kept: dense_path(
                tile_rows, index_rows, tile_count.reshape(()), history, drive, near_inverse, n_src, n_obs
            ),
            lambda kept: kept,
            both,
        )
        return both.transpose(0, 2, 1, 3).reshape(2, coefs, bd * width)

    in_specs = (
        P("src", "obs", None, None, None),
        P("src", "obs", None, None),
        P("src", "obs"),
        P(None, None, ("src", "obs")),
        P(None, None, ("src", "obs")),
        P(("src", "obs"), None, None),
    )
    out_specs = P(None, None, ("src", "obs"))
    return jax.shard_map(on_device, mesh=mesh, in_specs=in_specs, out_specs=out_specs, check_vma=False)
```

time: 538 us -> 117 us (0.22)
  waiting for transfers between devices: 298 us -> 0 us
  local copies, waits for them, and re-layouts: 124 us -> 3.43 us
  Pallas kernels: 0 us -> 109 us
  other arithmetic: 55.4 us -> 1.61 us
  matrix products: 40.1 us -> 0 us
  between operations: 13.2 us -> 1.4 us
    psum x2 -> x0, waiting for transfers between devices: 165 us -> none  [settle(): summed = lax.psum(partial_value, 'src')]
    all_gather x2 -> x0, waiting for transfers between devices: 133 us -> none  [the longest x1 96.2 us: on_device(): gathered = lax.all_gather(history, 'obs', axis=2, tiled=True)]
    gather x24 -> x0, local copies, waits for them, and re-layouts: 120 us -> none  [the longest x8 52.3 us: chooser_second(): older = history_src[jnp.maximum(delay_slot - 1, 0), :, source]]
    pallas_call x0 -> x6, Pallas kernels: none -> 109 us  [the longest x1 36.2 us: on_device(): pl.pallas_call(functools.partial(first_kernel, n_src, n_obs, bd), name='f...]
    scatter-add x16 -> x0, other arithmetic: 43.9 us -> none  [one_group(): return partial_value.at[:, index_part[0]].add(products)]
    dot_general x18 -> x0, matrix products: 40.1 us -> none  [the longest x16 36.3 us: one_group(): jnp.einsum('gck,gki->cgi', operand, tile_part, preferred_element_type=jnp...]
    lt x16 -> x0, other arithmetic: 10.5 us -> none  [one_group(): alive_mask = start + jnp.arange(group_size, dtype=jnp.int32) < live_count]
  transfers between devices with their start and end apart: 4 -> 0, of which waited for: 4 -> 0; matrix products, arithmetic and copies ran while one was open for 0% -> 0% of each run, Pallas kernels for 0% -> 0%
where the time goes in v1:
time: 117 us; the launch traced here: 116 us
  Pallas kernels  109 us (93%)
  local copies, waits for them, and re-layouts  3.43 us (3%)
  other arithmetic  1.61 us (1%)
  between operations  1.4 us (1%)
    pallas_call x1, Pallas kernels, on_device(): pl.pallas_call(functools.partial(first_kernel, n_src, n_obs, bd), name='f...  36.2 us
    pallas_call x2, Pallas kernels, products(): pl.pallas_call(functools.partial(products_kernel, which, chunk, depth), n...  21 us
    pallas_call x1, Pallas kernels, on_device(): pl.pallas_call(functools.partial(rows_kernel, n_src, n_obs, bd), name='ro...  20.7 us
    pallas_call x1, Pallas kernels, on_device(): pl.pallas_call(functools.partial(second_kernel, n_src, n_obs, bd), name='...  20.2 us
    pallas_call x1, Pallas kernels, on_device(): pl.pallas_call(functools.partial(request_kernel, n_src, n_obs, bd), name=...  10.9 us
    unnamed x10, local copies, waits for them, and re-layouts  2.73 us

profile of v1, /device:TPU:1, one launch (start us, length us, event | category | flops | bytes accessed | tf_op | source)
XLA Modules:
  0.0 115.6 jit_solution(10807606143901024226)
XLA Ops:
  0.0 0.0 copy-start.2
  0.0 0.0 copy-start
  0.0 1.4 %copy.70 = bf16[16,4,8192]{2,1,0:T(4,128)(2,1)S(1)} copy(bf16[16,4,8192]{2,1,0:T(4,128)(2,1)} %param.23) | data formatting | bytes 2097152
  2.0 0.7 copy.11
  2.7 10.9 %requests.1 = (s32[16,1,128]{2,1,0:T(1,128)}, s32[8,512]{1,0:T(8,128)}) custom-call(s32[3,512]{1,0:T(4,128)S(1)} %bitcast.132, s32[1,1]{1,0:T(1,128)S(6)} %copy.68.cnt_ref), custom_call_target="tpu_custom_call" | custom-call | tf_op jit(solution)/shard_map/requests/pallas_call | solution.py:360
  13.6 20.7 %rows.1 = (bf16[1024,4,128]{2,1,0:T(4,128)(2,1)}, s32[8,1,128]{2,1,0:T(1,128)}) custom-call(s32[16,1,128]{2,1,0:T(1,128)} %get-tuple-element.587.req_ref, bf16[1024,4,128]{2,1,0:T(4,128)(2,1)S(1)} %bitcast.125), custom_call_target="tpu_custom_call" | custom-call | tf_op jit(solution)/shard_map/rows/pallas_call | solution.py:373
  34.4 10.5 %products.2.part_ref = f32[520,4,128]{2,1,0:T(4,128)} custom-call(s32[8,512]{1,0:T(8,128)} %get-tuple-element.589.info_ref, s32[1,1]{1,0:T(1,128)S(6)} %copy.68.cnt_ref, bf16[512,128,128]{2,1,0:T(8,128)(2,1)} %bitcast.122, bf16[1024,4,128]{2,1,0:T(4,128)(2,1)} %get-tuple-element.590.rows_ref), custom_call_target="tpu_custom_call" | custom-call | tf_op jit(solution)/shard_map/products/pallas_call | solution.py:392
  44.8 0.0 copy-start.4
  44.8 0.0 copy-done.2
  44.8 0.7 slice_bitcast_fusion
  45.5 0.0 copy-done
  45.5 36.2 %first.1 = (bf16[64,4,128]{2,1,0:T(4,128)(2,1)}, bf16[1280,4,128]{2,1,0:T(4,128)(2,1)}) custom-call(s32[16,1,128]{2,1,0:T(1,128)} %get-tuple-element.587.req_ref, f32[520,4,128]{2,1,0:T(4,128)} %products.2.part_ref, f32[64,4,128]{2,1,0:T(4,128)} %get-tuple-element.654.inc_ref, bf16[64,128,128]{2,1,0:T(8,128)(2,1)S(1)} %copy-done, ...), custom_call_target="tpu_custom_call" | custom-call | tf_op jit(solution)/shard_map/first/pallas_call | solution.py:402
  81.7 10.5 %products.3.part_ref = f32[520,4,128]{2,1,0:T(4,128)} custom-call(s32[8,512]{1,0:T(8,128)} %get-tuple-element.589.info_ref, s32[1,1]{1,0:T(1,128)S(6)} %copy.68.cnt_ref, bf16[512,128,128]{2,1,0:T(8,128)(2,1)} %bitcast.123, bf16[1280,4,128]{2,1,0:T(4,128)(2,1)} %get-tuple-element.592.rows_ref), custom_call_target="tpu_custom_call" | custom-call | tf_op jit(solution)/shard_map/products/pallas_call | solution.py:392
  92.3 20.2 %second.1 = bf16[64,4,128]{2,1,0:T(4,128)(2,1)} custom-call(f32[520,4,128]{2,1,0:T(4,128)} %products.3.part_ref, f32[64,4,128]{2,1,0:T(4,128)} %get-tuple-element.653.inc_ref, bf16[64,128,128]{2,1,0:T(8,128)(2,1)S(1)} %copy-done), custom_call_target="tpu_custom_call" | custom-call | tf_op jit(solution)/shard_map/second/pallas_call | solution.py:422
  112.5 1.0 pad_maximum_fusion.1
  113.5 0.0 copy-done.4
  113.5 0.6 reduce_max.9
  114.8 0.2 conditional.1
  115.0 0.0 copy-start.3
  115.0 0.6 copy-done.3
Async XLA Ops:
  0.0 44.8 %copy-start.2 = (f32[2,4,8192]{2,1,0:T(4,128)S(1)}, f32[2,4,8192]{2,1,0:T(4,128)}, u32[]{:S(2)}) copy-start(f32[2,4,8192]{2,1,0:T(4,128)} %param.24) | copy-start | bytes 786436
  0.0 45.5 %copy-start = (bf16[64,128,128]{2,1,0:T(8,128)(2,1)S(1)}, bf16[64,128,128]{2,1,0:T(8,128)(2,1)}, u32[]{:S(2)}) copy-start(bf16[64,128,128]{2,1,0:T(8,128)(2,1)} %near_ref.3) | copy-start | bytes 6291460
  44.8 68.7 %copy-start.4 = (s32[8,1,128]{2,1,0:T(1,128)S(1)}, s32[8,1,128]{2,1,0:T(1,128)}, u32[]{:S(2)}) copy-start(s32[8,1,128]{2,1,0:T(1,128)} %get-tuple-element.588) | copy-start | bytes 12292
  115.0 0.7 copy-start.3

commit v2 on v1

--- a/solution.py
+++ b/solution.py
@@ -157,7 +157,7 @@
         copy.wait()
 
 
-def products_kernel(which, chunk, depth, info_ref, cnt_ref, tiles_ref, rows_ref, acc_ref, buf, sem):
+def products_kernel(which, chunk, depth, info_ref, cnt_ref, tiles_ref, rows_ref, out_ref, acc_ref, buf, sem):
     live = cnt_ref[0, 0]
     chunks = (live + chunk - 1) // chunk
 
@@ -187,6 +187,7 @@
         return carry
 
     lax.fori_loop(0, chunks, one_chunk, 0)
+    out_ref[...] = acc_ref[0 : out_ref.shape[0]].astype(jnp.bfloat16)
 
 
 def scatter_start(n_src, bd, part_ref, recv, send_sem, recv_sem):
@@ -206,9 +207,9 @@
 
     def one(turn, carry):
         at = pl.ds(turn * step, step)
-        total = part_ref[pl.ds(me_s * bd + turn * step, step)]
+        total = part_ref[pl.ds(me_s * bd + turn * step, step)].astype(jnp.float32)
         for k in range(1, n_src):
-            total = total + recv[k, at]
+            total = total + recv[k, at].astype(jnp.float32)
         drive = (inc_ref[at] - total).astype(jnp.bfloat16)
         for i in range(step):
             b = turn * step + i
@@ -392,10 +393,13 @@
             return pl.pallas_call(
                 functools.partial(products_kernel, which, chunk, depth),
                 name="products",
-                out_shape=jax.ShapeDtypeStruct((n_src * bd + 8, coefs, width), jnp.float32),
+                out_shape=jax.ShapeDtypeStruct((n_src * bd, coefs, width), jnp.bfloat16),
                 in_specs=[smem, smem, anywhere, vmem],
                 out_specs=vmem,
-                scratch_shapes=[pltpu.VMEM((depth, chunk, width, width), jnp.bfloat16), dma((depth,))],
+                scratch_shapes=[
+                    pltpu.VMEM((n_src * bd + 8, coefs, width), jnp.float32),
+                    pltpu.VMEM((depth, chunk, width, width), jnp.bfloat16), dma((depth,)),
+                ],
             )(info, tile_count, tile_rows, row_array)
 
         part = products(0, rows)
@@ -409,7 +413,7 @@
             in_specs=[smem, vmem, vmem, anywhere, vmem],
             out_specs=(vmem, anywhere),
             scratch_shapes=[
-                pltpu.VMEM((n_src, bd, coefs, width), jnp.float32),
+                pltpu.VMEM((n_src, bd, coefs, width), jnp.bfloat16),
                 pltpu.VMEM((bd, width, width), jnp.bfloat16),
                 pltpu.VMEM((n_obs, CAP, coefs, width), jnp.bfloat16),
                 pltpu.VMEM((n_obs, CAP0, coefs, width), jnp.bfloat16),
@@ -426,7 +430,7 @@
             in_specs=[vmem, vmem, anywhere],
             out_specs=vmem,
             scratch_shapes=[
-                pltpu.VMEM((n_src, bd, coefs, width), jnp.float32),
+                pltpu.VMEM((n_src, bd, coefs, width), jnp.bfloat16),
                 pltpu.VMEM((bd, width, width), jnp.bfloat16),
                 dma, dma((n_src,)), dma((n_src,)),
             ],

time: 117 us -> 104 us (0.89); the launches traced: 116 us -> 104 us
  Pallas kernels: 109 us -> 97.3 us
    pallas_call x2, Pallas kernels: 21 us -> 8.68 us  [products(): pl.pallas_call(functools.partial(products_kernel, which, chunk, depth), n...]
    pallas_call x1, Pallas kernels: 20.2 us -> 21.7 us  [on_device(): pl.pallas_call(functools.partial(second_kernel, n_src, n_obs, bd), name='...]
where the time goes in v2:
time: 104 us
  Pallas kernels  97.3 us (94%)
  local copies, waits for them, and re-layouts  3.46 us (3%)
  other arithmetic  1.61 us (2%)
  between operations  1.4 us (1%)
    pallas_call x1, Pallas kernels, on_device(): pl.pallas_call(functools.partial(first_kernel, n_src, n_obs, bd), name='f...  35.3 us
    pallas_call x1, Pallas kernels, on_device(): pl.pallas_call(functools.partial(second_kernel, n_src, n_obs, bd), name='...  21.7 us
    pallas_call x1, Pallas kernels, on_device(): pl.pallas_call(functools.partial(rows_kernel, n_src, n_obs, bd), name='ro...  20.7 us
    pallas_call x1, Pallas kernels, on_device(): pl.pallas_call(functools.partial(request_kernel, n_src, n_obs, bd), name=...  10.9 us
    pallas_call x2, Pallas kernels, products(): pl.pallas_call(functools.partial(products_kernel, which, chunk, depth), n...  8.68 us
    unnamed x10, local copies, waits for them, and re-layouts  2.73 us

profile of v2, /device:TPU:1, one launch (start us, length us, event | category | flops | bytes accessed | tf_op | source)
XLA Modules:
  0.0 104.0 jit_solution(8364722181498046770)
XLA Ops:
  0.0 0.0 copy-start.2
  0.0 0.0 copy-start
  0.0 1.4 %copy.70 = bf16[16,4,8192]{2,1,0:T(4,128)(2,1)S(1)} copy(bf16[16,4,8192]{2,1,0:T(4,128)(2,1)} %param.23) | data formatting | bytes 2097152
  2.0 0.7 copy.11
  2.7 10.9 %requests.1 = (s32[16,1,128]{2,1,0:T(1,128)}, s32[8,512]{1,0:T(8,128)}) custom-call(s32[3,512]{1,0:T(4,128)S(1)} %bitcast.132, s32[1,1]{1,0:T(1,128)S(6)} %copy.68.cnt_ref), custom_call_target="tpu_custom_call" | custom-call | tf_op jit(solution)/shard_map/requests/pallas_call | solution.py:361
  13.7 20.7 %rows.1 = (bf16[1024,4,128]{2,1,0:T(4,128)(2,1)}, s32[8,1,128]{2,1,0:T(1,128)}) custom-call(s32[16,1,128]{2,1,0:T(1,128)} %get-tuple-element.587.req_ref, bf16[1024,4,128]{2,1,0:T(4,128)(2,1)S(1)} %bitcast.125), custom_call_target="tpu_custom_call" | custom-call | tf_op jit(solution)/shard_map/rows/pallas_call | solution.py:374
  34.4 4.3 %products.2.part_ref = bf16[512,4,128]{2,1,0:T(4,128)(2,1)} custom-call(s32[8,512]{1,0:T(8,128)} %get-tuple-element.589.info_ref, s32[1,1]{1,0:T(1,128)S(6)} %copy.68.cnt_ref, bf16[512,128,128]{2,1,0:T(8,128)(2,1)} %bitcast.122, bf16[1024,4,128]{2,1,0:T(4,128)(2,1)} %get-tuple-element.590.rows_ref), custom_call_target="tpu_custom_call" | custom-call | tf_op jit(solution)/shard_map/products/pallas_call | solution.py:393
  38.7 0.0 copy-start.4
  38.7 0.0 copy-done.2
  38.7 0.7 slice_bitcast_fusion
  39.4 0.0 copy-done
  39.4 35.3 %first.1 = (bf16[64,4,128]{2,1,0:T(4,128)(2,1)}, bf16[1280,4,128]{2,1,0:T(4,128)(2,1)}) custom-call(s32[16,1,128]{2,1,0:T(1,128)} %get-tuple-element.587.req_ref, bf16[512,4,128]{2,1,0:T(4,128)(2,1)} %products.2.part_ref, f32[64,4,128]{2,1,0:T(4,128)} %get-tuple-element.654.inc_ref, bf16[64,128,128]{2,1,0:T(8,128)(2,1)S(1)} %copy-done, ...), custom_call_target="tpu_custom_call" | custom-call | tf_op jit(solution)/shard_map/first/pallas_call | solution.py:406
  74.7 4.4 %products.3.part_ref = bf16[512,4,128]{2,1,0:T(4,128)(2,1)} custom-call(s32[8,512]{1,0:T(8,128)} %get-tuple-element.589.info_ref, s32[1,1]{1,0:T(1,128)S(6)} %copy.68.cnt_ref, bf16[512,128,128]{2,1,0:T(8,128)(2,1)} %bitcast.123, bf16[1280,4,128]{2,1,0:T(4,128)(2,1)} %get-tuple-element.592.rows_ref), custom_call_target="tpu_custom_call" | custom-call | tf_op jit(solution)/shard_map/products/pallas_call | solution.py:393
  79.1 21.7 %second.1 = bf16[64,4,128]{2,1,0:T(4,128)(2,1)} custom-call(bf16[512,4,128]{2,1,0:T(4,128)(2,1)} %products.3.part_ref, f32[64,4,128]{2,1,0:T(4,128)} %get-tuple-element.653.inc_ref, bf16[64,128,128]{2,1,0:T(8,128)(2,1)S(1)} %copy-done), custom_call_target="tpu_custom_call" | custom-call | tf_op jit(solution)/shard_map/second/pallas_call | solution.py:426
  100.9 1.0 pad_maximum_fusion.1
  101.8 0.0 copy-done.4
  101.8 0.6 reduce_max.9
  103.1 0.2 conditional.1
  103.3 0.0 copy-start.3
  103.3 0.6 copy-done.3
Async XLA Ops:
  0.0 38.7 %copy-start.2 = (f32[2,4,8192]{2,1,0:T(4,128)S(1)}, f32[2,4,8192]{2,1,0:T(4,128)}, u32[]{:S(2)}) copy-start(f32[2,4,8192]{2,1,0:T(4,128)} %param.24) | copy-start | bytes 786436
  0.0 39.4 %copy-start = (bf16[64,128,128]{2,1,0:T(8,128)(2,1)S(1)}, bf16[64,128,128]{2,1,0:T(8,128)(2,1)}, u32[]{:S(2)}) copy-start(bf16[64,128,128]{2,1,0:T(8,128)(2,1)} %near_ref.3) | copy-start | bytes 6291460
  38.7 63.2 %copy-start.4 = (s32[8,1,128]{2,1,0:T(1,128)S(1)}, s32[8,1,128]{2,1,0:T(1,128)}, u32[]{:S(2)}) copy-start(s32[8,1,128]{2,1,0:T(1,128)} %get-tuple-element.588) | copy-start | bytes 12292
  103.3 0.7 copy-start.3

commit v3 on v0

v3 whole, which is shorter than its diff:
```python
import functools

import jax
import jax.numpy as jnp
from jax import lax
from jax.experimental import pallas as pl
from jax.experimental.pallas import tpu as pltpu
from jax.sharding import PartitionSpec as P

MESH = pl.DeviceIdType.MESH
CAP = 64
CAP0 = 16
CAPD = 64
FAR = -(1 << 20)


def greet(src_peers, obs_peers, n_src, n_obs):
    me_s, me_o = lax.axis_index("src"), lax.axis_index("obs")
    barrier = pltpu.get_barrier_semaphore()
    if src_peers:
        for k in range(1, n_src):
            pl.semaphore_signal(
                barrier, inc=1, device_id=(lax.rem(me_s + k, n_src), me_o), device_id_type=MESH
            )
    if obs_peers:
        for k in range(1, n_obs):
            pl.semaphore_signal(
                barrier, inc=1, device_id=(me_s, lax.rem(me_o + k, n_obs)), device_id_type=MESH
            )
    total = (n_src - 1) * src_peers + (n_obs - 1) * obs_peers
    return lambda: pl.semaphore_wait(barrier, total)


def to_obs(k, n_obs, src_ref, dst_ref, send_sem, recv_sem):
    me_s, me_o = lax.axis_index("src"), lax.axis_index("obs")
    return pltpu.make_async_remote_copy(
        src_ref=src_ref, dst_ref=dst_ref, send_sem=send_sem.at[k], recv_sem=recv_sem.at[k],
        device_id=(me_s, lax.rem(me_o + k, n_obs)), device_id_type=MESH,
    )


def to_src(k, n_src, src_ref, dst_ref, send_sem, recv_sem):
    me_s, me_o = lax.axis_index("src"), lax.axis_index("obs")
    return pltpu.make_async_remote_copy(
        src_ref=src_ref, dst_ref=dst_ref, send_sem=send_sem.at[k], recv_sem=recv_sem.at[k],
        device_id=(lax.rem(me_s + k, n_src), me_o), device_id_type=MESH,
    )


def each(count, body, start=0):
    lax.fori_loop(start, count, lambda i, carry: (body(i), carry)[1], 0)


def request_kernel(n_src, n_obs, bd, idx_ref, cnt_ref, recv_ref, info_ref, list_ref, send_ref, send_sem, recv_sem):
    me = lax.axis_index("obs")
    entered = greet(0, 1, n_src, n_obs)
    n_tiles = idx_ref.shape[2]
    shift = bd.bit_length() - 1
    lane = lax.broadcasted_iota(jnp.int32, (1, n_tiles), 1)
    live = lane < cnt_ref[0, 0]
    obs_block, source, delay = idx_ref[0], idx_ref[1], idx_ref[2]
    owner = lax.shift_right_logical(source, shift)
    place = jnp.bitwise_and(source, bd - 1)
    owner_row = lax.broadcasted_iota(jnp.int32, (n_obs, n_tiles), 0)
    mine = jnp.where(jnp.logical_and(owner == owner_row, live), 1.0, 0.0)
    mine0 = jnp.where(delay == 0, mine, 0.0)
    before = jnp.where(
        lax.broadcasted_iota(jnp.int32, (n_tiles, n_tiles), 0)
        < lax.broadcasted_iota(jnp.int32, (n_tiles, n_tiles), 1),
        1.0, 0.0,
    ).astype(jnp.bfloat16)
    both = jnp.concatenate([mine, mine0], axis=0).astype(jnp.bfloat16)
    order = jnp.dot(both, before, preferred_element_type=jnp.float32)
    rank = jnp.sum(order[:n_obs] * mine, axis=0, keepdims=True)
    rank0 = jnp.sum(order[n_obs:] * mine0, axis=0, keepdims=True)
    rank_d = jnp.sum(order[n_obs:], axis=0, keepdims=True)
    newest = jnp.logical_and(live, delay == 0)
    over = jnp.where(live, jnp.where(rank >= CAP, 1.0, 0.0), 0.0) + jnp.where(
        newest, jnp.where(rank0 >= CAP0, 1.0, 0.0) + jnp.where(rank_d >= CAPD, 1.0, 0.0), 0.0
    )
    flag = jnp.max(over, axis=1, keepdims=True)
    rank = rank.astype(jnp.int32)
    rank0 = rank0.astype(jnp.int32)
    fits = jnp.logical_and(live, rank < CAP)
    fits0 = jnp.logical_and(newest, rank0 < CAP0)
    nowhere = n_src * bd
    info_ref[0:1, :] = jnp.where(fits, owner * CAP + rank, 0)
    info_ref[1:2, :] = jnp.where(live, obs_block, nowhere)
    info_ref[2:3, :] = jnp.where(jnp.logical_and(live, delay > 0), obs_block, nowhere)
    info_ref[3:8, :] = jnp.zeros((5, n_tiles), jnp.int32)
    key = jnp.where(fits, owner * 128 + rank, FAR)
    key0 = jnp.where(fits0, owner * 128 + CAP + rank0, FAR)
    key_d = jnp.where(newest, rank_d.astype(jnp.int32), FAR)
    code_row = lax.broadcasted_iota(jnp.int32, (16, n_tiles), 0)
    codes = jnp.zeros((16, n_tiles), jnp.int32)
    slot0 = jnp.where(fits0, owner * CAP0 + rank0, 0)
    parts = (
        place, delay, jnp.bitwise_and(lane, 127), lax.shift_right_logical(lane, 7), slot0,
        jnp.bitwise_and(obs_block, 127), lax.shift_right_logical(obs_block, 7), jnp.ones_like(lane),
    )
    for i, part in enumerate(parts):
        codes = jnp.where(code_row == i, part, codes)
    codes = codes.astype(jnp.float32).astype(jnp.bfloat16)
    row = lax.broadcasted_iota(jnp.int32, (128, n_tiles), 0)
    out_lane = lax.broadcasted_iota(jnp.int32, (1, 128), 1)

    def find(hit):
        pick = jnp.where(hit, 1.0, 0.0).astype(jnp.bfloat16)
        return lax.dot_general(codes, pick, (((1,), (1,)), ((), ())), preferred_element_type=jnp.float32)

    def one_owner(o):
        found = find(jnp.logical_or(key - o * 128 == row, key0 - o * 128 == row))
        code = found[0:1, :] + found[1:2, :] * bd
        send_ref[o] = jnp.where(out_lane == 127, flag, code).astype(jnp.int32)

    each(n_obs, one_owner)
    recv_ref[me] = send_ref[me]
    entered()

    def send(k):
        return to_obs(k, n_obs, send_ref.at[lax.rem(me + k, n_obs)], recv_ref.at[me], send_sem, recv_sem)

    each(n_obs, lambda k: send(k).start(), 1)
    found = find(key_d == row)
    list_ref[0:1, :] = (found[2:3, :] + found[3:4, :] * 128.0).astype(jnp.int32)
    list_ref[1:2, :] = found[4:5, :].astype(jnp.int32)
    list_ref[2:3, :] = jnp.where(found[7:8, :] > 0.5, found[5:6, :] + found[6:7, :] * 128.0, 1.0 * nowhere).astype(jnp.int32)
    list_ref[3:8, :] = jnp.zeros((5, 128), jnp.int32)
    each(n_obs, lambda k: send(k).wait(), 1)


def step_kernel(
    n_src, n_obs, bd, req, info, lst, info_v, list_v, tiles_ref, hist_ref, inc_ref, near_ref,
    out_ref, flags_ref,
    tile, hist, inc, near, rows1, rows2, rows0, send1, send2, send0, mark,
    y_one, y_high, y_rest, y_new, pick1, pick2, pick0, part_old, part1, part2, recv1, recv2, drive,
    tile_sem, load_sem, fsend, frecv, send_sem1, recv_sem1, send_sem2, recv_sem2, send_sem0, recv_sem0,
    rsend1, rrecv1, rsend2, rrecv2,
):
    me_s, me_o = lax.axis_index("src"), lax.axis_index("obs")
    entered = greet(1, 1, n_src, n_obs)
    n_tiles = tiles_ref.shape[0]
    chunks = tile_sem.shape[0]
    chunk = n_tiles // chunks
    width = tiles_ref.shape[2]
    coefs = hist_ref.shape[1]
    blocks = n_src * bd
    load_hist = pltpu.make_async_copy(hist_ref, hist, load_sem.at[0])
    load_near = pltpu.make_async_copy(near_ref, near, load_sem.at[1])
    load_inc = pltpu.make_async_copy(inc_ref, inc, load_sem.at[2])

    def load_tiles(c):
        at = pl.ds(c * chunk, chunk)
        return pltpu.make_async_copy(tiles_ref.at[at], tile.at[at], tile_sem.at[c])

    load_hist.start()
    flag = req[0, 0, 127]
    for o in range(1, n_obs):
        flag = jnp.maximum(flag, req[o, 0, 127])
    mark[...] = jnp.full(mark.shape, flag, jnp.int32)
    flags_ref[me_s] = mark[...]

    def gather(table, out, o, slots, first, code_to_row):
        def eight(turn):
            for i in range(8):
                r = turn * 8 + i
                out[r] = table[code_to_row(req[o, 0, first + r])]

        each(slots // 8, eight)

    def send_flag(k):
        return to_src(k, n_src, mark, flags_ref.at[me_s], fsend, frecv)

    def send_rows(k, send, rows, cap, send_sem, recv_sem):
        return to_obs(k, n_obs, send.at[k], rows.at[pl.ds(me_o * cap, cap)], send_sem, recv_sem)

    def one_dest(k):
        gather(hist, send1.at[k], lax.rem(me_o + k, n_obs), CAP, 0, lambda c: c)

    def send_one(k):
        return send_rows(k, send1, rows1, CAP, send_sem1, recv_sem1)

    load_hist.wait()
    one_dest(1)
    load_inc.start()
    load_near.start()
    each(chunks, lambda c: load_tiles(c).start())
    entered()
    send_one(1).start()

    def gather_send(k):
        one_dest(k)
        send_one(k).start()

    each(n_obs, gather_send, 2)
    each(n_src, lambda k: send_flag(k).start(), 1)
    gather(hist, rows1.at[pl.ds(me_o * CAP, CAP)], me_o, CAP, 0, lambda c: c)

    older = lambda c: jnp.maximum(c - bd, 0)
    each(n_obs, lambda k: gather(hist, send2.at[k], lax.rem(me_o + k, n_obs), CAP, 0, older), 1)
    gather(hist, rows2.at[pl.ds(me_o * CAP, CAP)], me_o, CAP, 0, older)

    row = lax.broadcasted_iota(jnp.int32, (bd, n_tiles), 0)
    row0 = lax.broadcasted_iota(jnp.int32, (bd, CAPD), 0)

    def one_pick(j):
        at = pl.ds(j * bd, bd)
        ones = lambda hit: jnp.where(hit, 1.0, 0.0).astype(jnp.bfloat16)
        pick1[j] = ones(info_v[1:2, :] - j * bd == row)
        pick2[j] = ones(info_v[2:3, :] - j * bd == row)
        pick0[j] = ones(list_v[2:3, 0:CAPD] - j * bd == row0)

    each(n_src, one_pick)

    def two_products(x0, x1, t0, t1, y, count, at):
        x = jnp.concatenate([x0.astype(jnp.float32), x1.astype(jnp.float32)], axis=0).astype(jnp.bfloat16)
        both = jnp.dot(x, jnp.concatenate([t0, t1], axis=1), preferred_element_type=jnp.float32)
        y[pl.ds(at, coefs, stride=count), :] = both[:coefs, :width]
        y[pl.ds(at + 1, coefs, stride=count), :] = both[coefs:, width:]

    def products(rows):
        def one_chunk(c):
            for i in range(0, chunk, 2):
                t = c * chunk + i
                two_products(rows[info[0, t]], rows[info[0, t + 1]], tile[t], tile[t + 1], y_one, n_tiles, t)

        return one_chunk

    def split():
        for c in range(coefs):
            lanes = slice(c * width, (c + 1) * width)

            def some(i):
                at = pl.multiple_of(i * 64, 64)
                value = y_one[pl.ds(c * n_tiles + at, 64), :]
                high = value.astype(jnp.bfloat16)
                y_high[pl.ds(at, 64), lanes] = high
                y_rest[pl.ds(at, 64), lanes] = (value - high.astype(jnp.float32)).astype(jnp.bfloat16)

            each(n_tiles // 64, some)

    def add_up(pick):
        return jnp.dot(pick, y_high[...], preferred_element_type=jnp.float32) + jnp.dot(
            pick, y_rest[...], preferred_element_type=jnp.float32
        )

    def send_part(k, part, recv, send_sem, recv_sem):
        return to_src(k, n_src, part.at[lax.rem(me_s + k, n_src)], recv.at[me_s], send_sem, recv_sem)

    def solve(which, recv, part):
        total = part[me_s].astype(jnp.float32)
        for k in range(1, n_src):
            total = total + recv[lax.rem(me_s + k, n_src)].astype(jnp.float32)
        for c in range(coefs):
            drive[pl.ds(c * bd, bd), :] = total[:, c * width : (c + 1) * width]

        def pairs(turn):
            for i in range(4):
                b = turn * 8 + 2 * i
                x0 = inc[which, b] - drive[pl.ds(b, coefs, stride=bd), :]
                x1 = inc[which, b + 1] - drive[pl.ds(b + 1, coefs, stride=bd), :]
                x = jnp.concatenate([x0, x1], axis=0).astype(jnp.bfloat16)
                both = jnp.dot(
                    x, jnp.concatenate([near[b], near[b + 1]], axis=1), preferred_element_type=jnp.float32
                )
                out_ref[which, b] = both[:coefs, :width].astype(jnp.bfloat16)
                out_ref[which, b + 1] = both[coefs:, width:].astype(jnp.bfloat16)

        each(bd // 8, pairs)

    send_two = lambda k: send_rows(k, send2, rows2, CAP, send_sem2, recv_sem2)
    each(chunks, lambda c: load_tiles(c).wait())
    each(n_obs, lambda k: send_one(k).wait(), 1)
    each(n_obs, lambda k: send_two(k).start(), 1)
    each(chunks, products(rows1))
    split()
    part_one = lambda k: send_part(k, part1, recv1, rsend1, rrecv1)

    def sum_send_one(k):
        j = lax.rem(me_s + k, n_src)
        part1[j] = add_up(pick1[j]).astype(jnp.bfloat16)
        part_one(k).start()

    each(n_src, sum_send_one, 1)
    part1[me_s] = add_up(pick1[me_s]).astype(jnp.bfloat16)
    load_inc.wait()
    load_near.wait()
    each(n_src, lambda k: part_one(k).wait(), 1)
    solve(0, recv1, part1)

    newest = out_ref.at[0]
    placed = lambda c: jnp.bitwise_and(c, bd - 1)
    send_new = lambda k: send_rows(k, send0, rows0, CAP0, send_sem0, recv_sem0)

    def gather_send_new(k):
        gather(newest, send0.at[k], lax.rem(me_o + k, n_obs), CAP0, CAP, placed)
        send_new(k).start()

    each(n_obs, gather_send_new, 1)
    gather(newest, rows0.at[pl.ds(me_o * CAP0, CAP0)], me_o, CAP0, CAP, placed)
    each(n_obs, lambda k: send_two(k).wait(), 1)
    each(chunks, products(rows2))
    split()

    def sum_old(j):
        part_old[j] = add_up(pick2[j])

    each(n_src, sum_old)
    each(n_obs, lambda k: send_new(k).wait(), 1)

    def new_products(turn):
        for i in range(0, 8, 2):
            r = turn * 8 + i
            two_products(
                rows0[lst[1, r]], rows0[lst[1, r + 1]], tile[lst[0, r]], tile[lst[0, r + 1]], y_new, CAPD, r
            )

    each(CAPD // 8, new_products)
    value = jnp.concatenate([y_new[c * CAPD : (c + 1) * CAPD, :] for c in range(coefs)], axis=1)
    high = value.astype(jnp.bfloat16)
    rest = (value - high.astype(jnp.float32)).astype(jnp.bfloat16)
    part_two = lambda k: send_part(k, part2, recv2, rsend2, rrecv2)

    def sum_two(j):
        added = jnp.dot(pick0[j], high, preferred_element_type=jnp.float32) + jnp.dot(
            pick0[j], rest, preferred_element_type=jnp.float32
        )
        part2[j] = (part_old[j] + added).astype(jnp.bfloat16)

    def sum_send_two(k):
        sum_two(lax.rem(me_s + k, n_src))
        part_two(k).start()

    each(n_src, sum_send_two, 1)
    sum_two(me_s)
    each(n_src, lambda k: part_two(k).wait(), 1)
    solve(1, recv2, part2)
    each(n_src, lambda k: send_flag(k).wait(), 1)


def dense_path(tile_rows, index_rows, live_count, history, incident, near_inverse, n_src, n_obs):
    bd, width = near_inverse.shape[:2]
    slots, coefs = history.shape[:2]
    n_tiles = tile_rows.shape[0]
    group = min(64, n_tiles)

    def gather_obs(block):
        ring = [(i, (i + 1) % n_obs) for i in range(n_obs)]
        me = lax.axis_index("obs")
        whole = jnp.zeros((n_obs,) + block.shape, block.dtype)

        def hop(k, carry):
            whole, moving = carry
            whole = lax.dynamic_update_index_in_dim(whole, moving, lax.rem(me - k + n_obs, n_obs), 0)
            return whole, lax.ppermute(moving, "obs", ring)

        return lax.fori_loop(0, n_obs, hop, (whole, block))[0]

    def sum_src(value):
        ring = [(i, (i + 1) % n_src) for i in range(n_src)]

        def hop(k, carry):
            total, moving = carry
            moving = lax.ppermute(moving, "src", ring)
            return total + moving, moving

        return lax.fori_loop(0, n_src - 1, hop, (value, value))[0]

    def accumulate(chooser):
        def one_group(turn, partial):
            start = turn * group
            tile_part = lax.dynamic_slice_in_dim(tile_rows, start, group, 0)
            index_part = lax.dynamic_slice_in_dim(index_rows, start, group, 1)
            products = jnp.einsum(
                "gck,gki->gci", chooser(index_part), tile_part, preferred_element_type=jnp.float32
            )
            alive = start + jnp.arange(group, dtype=jnp.int32) < live_count
            products = jnp.where(alive[:, None, None], products, 0.0)
            return partial.at[index_part[0]].add(products)

        initial = jnp.zeros((bd * n_src, coefs, width), jnp.float32)
        return lax.fori_loop(0, n_tiles // group, one_group, initial)

    def settle(partial, drive):
        own = lax.dynamic_slice_in_dim(sum_src(partial), lax.axis_index("src") * bd, bd, 0)
        right = (drive - own).astype(jnp.bfloat16)
        solved = jnp.einsum("bck,bki->bci", right, near_inverse, preferred_element_type=jnp.float32)
        return solved.astype(jnp.bfloat16)

    past = gather_obs(history)

    def pick(block, index_part, slot):
        return past[index_part[1] // bd, slot, index_part[1] % bd]

    past = past.reshape(n_obs, slots, coefs, bd, width).transpose(0, 1, 3, 2, 4)
    first = settle(accumulate(lambda ip: pick(past, ip, ip[2])), incident[0])
    newest = gather_obs(first)

    def second_rows(ip):
        older = pick(past, ip, jnp.maximum(ip[2] - 1, 0))
        newer = newest[ip[1] // bd, ip[1] % bd]
        return jnp.where((ip[2] == 0)[:, None, None], newer, older)

    second = settle(accumulate(second_rows), incident[1])
    return jnp.stack([first, second])


def solution(mesh):
    n_src, n_obs = mesh.shape["src"], mesh.shape["obs"]
    vmem = pl.BlockSpec(memory_space=pltpu.VMEM)
    smem = pl.BlockSpec(memory_space=pltpu.SMEM)
    anywhere = pl.BlockSpec(memory_space=pl.ANY)
    dma = pltpu.SemaphoreType.DMA
    f32, bf16, i32 = jnp.float32, jnp.bfloat16, jnp.int32

    def params(i):
        return pltpu.CompilerParams(collective_id=i, has_side_effects=True)

    def on_device(tiles, tile_index, tile_count, history, incident, near_inverse):
        n_tiles, width = tiles.shape[2], tiles.shape[4]
        bd = near_inverse.shape[0]
        slots, coefs = history.shape[:2]
        tile_rows = tiles.reshape(n_tiles, width, width)
        index_rows = tile_index.transpose(0, 2, 1, 3).reshape(3, 1, n_tiles)
        hist = history.reshape(slots, coefs, bd, width).transpose(0, 2, 1, 3).reshape(slots * bd, coefs, width)
        drive = incident.reshape(2, coefs, bd, width).transpose(0, 2, 1, 3)

        requests, info, newest = pl.pallas_call(
            functools.partial(request_kernel, n_src, n_obs, bd),
            name="requests",
            out_shape=(
                jax.ShapeDtypeStruct((n_obs, 1, 128), i32),
                jax.ShapeDtypeStruct((8, n_tiles), i32),
                jax.ShapeDtypeStruct((8, 128), i32),
            ),
            in_specs=[vmem, smem],
            out_specs=(vmem, vmem, vmem),
            scratch_shapes=[pltpu.VMEM((n_obs, 1, 128), i32), dma((n_obs,)), dma((n_obs,))],
            compiler_params=params(0),
        )(index_rows, tile_count)

        def rows(cap):
            return pltpu.VMEM((n_obs * cap, coefs, width), bf16)

        def sends(cap):
            return pltpu.VMEM((n_obs, cap, coefs, width), bf16)

        def parts(kind):
            return pltpu.VMEM((n_src, bd, coefs * width), kind)

        chunks = max(1, n_tiles // 32)
        both, flags = pl.pallas_call(
            functools.partial(step_kernel, n_src, n_obs, bd),
            name="step",
            out_shape=(
                jax.ShapeDtypeStruct((2, bd, coefs, width), bf16),
                jax.ShapeDtypeStruct((n_src, 1, 128), i32),
            ),
            in_specs=[smem, smem, smem, vmem, vmem, anywhere, anywhere, anywhere, anywhere],
            out_specs=(vmem, vmem),
            scratch_shapes=[
                pltpu.VMEM((n_tiles, width, width), bf16),
                pltpu.VMEM(hist.shape, bf16),
                pltpu.VMEM(drive.shape, f32),
                pltpu.VMEM((bd, width, width), bf16),
                rows(CAP), rows(CAP), rows(CAP0), sends(CAP), sends(CAP), sends(CAP0),
                pltpu.VMEM((1, 128), i32),
                pltpu.VMEM((coefs * n_tiles, width), f32),
                pltpu.VMEM((n_tiles, coefs * width), bf16),
                pltpu.VMEM((n_tiles, coefs * width), bf16),
                pltpu.VMEM((coefs * CAPD, width), f32),
                pltpu.VMEM((n_src, bd, n_tiles), bf16),
                pltpu.VMEM((n_src, bd, n_tiles), bf16),
                pltpu.VMEM((n_src, bd, CAPD), bf16),
                parts(f32), parts(bf16), parts(bf16), parts(bf16), parts(bf16),
                pltpu.VMEM((coefs * bd, width), f32),
                dma((chunks,)), dma((3,)),
                dma((n_src,)), dma((n_src,)),
                dma((n_obs,)), dma((n_obs,)), dma((n_obs,)), dma((n_obs,)), dma((n_obs,)), dma((n_obs,)),
                dma((n_src,)), dma((n_src,)), dma((n_src,)), dma((n_src,)),
            ],
            compiler_params=params(1),
        )(requests, info, newest, info, newest, tile_rows, hist, drive, near_inverse)
        crowded = jnp.max(flags) > 0

        both = lax.cond(
            crowded,
            lambda kept: dense_path(
                tile_rows, tile_index.reshape(3, n_tiles), tile_count.reshape(()), history, drive, near_inverse,
                n_src, n_obs,
            ),
            lambda kept: kept,
            both,
        )
        return both.transpose(0, 2, 1, 3).reshape(2, coefs, bd * width)

    in_specs = (
        P("src", "obs", None, None, None),
        P("src", "obs", None, None),
        P("src", "obs"),
        P(None, None, ("src", "obs")),
        P(None, None, ("src", "obs")),
        P(("src", "obs"), None, None),
    )
    out_specs = P(None, None, ("src", "obs"))
    return jax.shard_map(on_device, mesh=mesh, in_specs=in_specs, out_specs=out_specs, check_vma=False)
```

time: 538 us -> 80 us (0.15); the launches traced: 531 us -> 79.7 us
  waiting for transfers between devices: 298 us -> 0 us
  local copies, waits for them, and re-layouts: 124 us -> 1.93 us
  Pallas kernels: 0 us -> 75.1 us
  other arithmetic: 55.4 us -> 1.32 us
  matrix products: 40.1 us -> 0 us
  between operations: 13.2 us -> 1.35 us
    psum x2 -> x0, waiting for transfers between devices: 165 us -> none  [settle(): summed = lax.psum(partial_value, 'src')]
    all_gather x2 -> x0, waiting for transfers between devices: 133 us -> none  [the longest x1 96.2 us: on_device(): gathered = lax.all_gather(history, 'obs', axis=2, tiled=True)]
    gather x24 -> x0, local copies, waits for them, and re-layouts: 120 us -> none  [the longest x8 52.3 us: chooser_second(): older = history_src[jnp.maximum(delay_slot - 1, 0), :, source]]
    pallas_call x0 -> x2, Pallas kernels: none -> 75.1 us  [the longest x1 63.5 us: on_device(): pl.pallas_call(functools.partial(step_kernel, n_src, n_obs, bd), name='st...]
    scatter-add x16 -> x0, other arithmetic: 43.9 us -> none  [one_group(): return partial_value.at[:, index_part[0]].add(products)]
    dot_general x18 -> x0, matrix products: 40.1 us -> none  [the longest x16 36.3 us: one_group(): jnp.einsum('gck,gki->cgi', operand, tile_part, preferred_element_type=jnp...]
    lt x16 -> x0, other arithmetic: 10.5 us -> none  [one_group(): alive_mask = start + jnp.arange(group_size, dtype=jnp.int32) < live_count]
  transfers between devices with their start and end apart: 4 -> 0, of which waited for: 4 -> 0; matrix products, arithmetic and copies ran while one was open for 0% -> 0% of each run, Pallas kernels for 0% -> 0%
where the time goes in v3:
time: 80 us; the launch traced here: 79.7 us
  Pallas kernels  75.1 us (94%)
  local copies, waits for them, and re-layouts  1.93 us (2%)
  between operations  1.35 us (2%)
  other arithmetic  1.32 us (2%)
    pallas_call x1, Pallas kernels, on_device(): pl.pallas_call(functools.partial(step_kernel, n_src, n_obs, bd), name='st...  63.5 us
    pallas_call x1, Pallas kernels, on_device(): pl.pallas_call(functools.partial(request_kernel, n_src, n_obs, bd), name=...  11.6 us
    unnamed x6, local copies, waits for them, and re-layouts  1.93 us

profile of v3, /device:TPU:1, one launch (start us, length us, event | category | flops | bytes accessed | tf_op | source)
XLA Modules:
  0.0 79.7 jit_solution(411492405162370230)
XLA Ops:
  0.0 0.0 copy-start.1
  0.0 0.0 copy-start
  0.0 1.3 %copy.71 = bf16[16,4,8192]{2,1,0:T(4,128)(2,1)S(1)} copy(bf16[16,4,8192]{2,1,0:T(4,128)(2,1)} %param.23) | data formatting | bytes 2097152
  1.9 11.6 %requests.1 = (s32[16,1,128]{2,1,0:T(1,128)}, s32[8,512]{1,0:T(8,128)}, s32[8,128]{1,0:T(8,128)}) custom-call(s32[3,1,512]{2,1,0:T(1,128)} %bitcast.126, s32[1,1]{1,0:T(1,128)S(6)} %copy.69.cnt_ref), custom_call_target="tpu_custom_call" | custom-call | tf_op jit(solution)/shard_map/requests/pallas_call | solution.py:428
  13.5 63.5 %step.1 = (bf16[2,64,4,128]{3,2,1,0:T(4,128)(2,1)S(1)}, s32[8,1,128]{2,1,0:T(1,128)}) custom-call(s32[16,1,128]{2,1,0:T(1,128)} %get-tuple-element.586.req, s32[8,512]{1,0:T(8,128)} %get-tuple-element.587.info.info_v, s32[8,128]{1,0:T(8,128)} %get-tuple-element.588.lst.list_v, s32[8,512]{1,0:T(8,128)} %get-tuple-element.587.info.info_v, ...), custom_call_target="tpu_custom_call" | custom-call | tf_op jit(solution)/shard_map/step/pallas_call | solution.py:452
  77.0 1.3 %reduce_max.9 = s32[]{:T(128)} reduce(s32[8,1,128]{2,1,0:T(1,128)} %get-tuple-element.589, s32[]{:T(128)} %constant.322.clone.1), dimensions={0,1,2}, to_apply=%region_0.0 | reduce | flops 1023 | bytes 4104 | tf_op jit(solution)/shard_map/reduce_max | solution.py:484
  79.0 0.0 copy-done.1
  79.0 0.0 copy-done
  79.0 0.7 copy.72
  (1 shorter events, 0.0 us)
Async XLA Ops:
  0.0 79.0 %copy-start.1 = (s32[1,1,3,512]{3,1,2,0:T(1,128)S(1)}, s32[1,1,3,512]{3,1,2,0:T(1,128)}, u32[]{:S(2)}) copy-start(s32[1,1,3,512]{3,1,2,0:T(1,128)} %param.21) | copy-start | bytes 18436
  0.0 79.0 %copy-start = (f32[2,4,8192]{2,1,0:T(4,128)S(1)}, f32[2,4,8192]{2,1,0:T(4,128)}, u32[]{:S(2)}) copy-start(f32[2,4,8192]{2,1,0:T(4,128)} %param.24) | copy-start | bytes 786436

commit v4 on v3

--- a/solution.py
+++ b/solution.py
@@ -8,10 +8,11 @@
 from jax.sharding import PartitionSpec as P
 
 MESH = pl.DeviceIdType.MESH
-CAP = 64
-CAP0 = 16
+CAP = 60
+CAP0 = 12
 CAPD = 64
 FAR = -(1 << 20)
+AT0 = 64
 
 
 def greet(src_peers, obs_peers, n_src, n_obs):
@@ -51,9 +52,7 @@
     lax.fori_loop(start, count, lambda i, carry: (body(i), carry)[1], 0)
 
 
-def request_kernel(n_src, n_obs, bd, idx_ref, cnt_ref, recv_ref, info_ref, list_ref, send_ref, send_sem, recv_sem):
-    me = lax.axis_index("obs")
-    entered = greet(0, 1, n_src, n_obs)
+def build_requests(n_src, n_obs, bd, rows, idx_ref, cnt_ref, send_ref, info_ref, list_ref):
     n_tiles = idx_ref.shape[2]
     shift = bd.bit_length() - 1
     lane = lax.broadcasted_iota(jnp.int32, (1, n_tiles), 1)
@@ -78,64 +77,63 @@
     over = jnp.where(live, jnp.where(rank >= CAP, 1.0, 0.0), 0.0) + jnp.where(
         newest, jnp.where(rank0 >= CAP0, 1.0, 0.0) + jnp.where(rank_d >= CAPD, 1.0, 0.0), 0.0
     )
-    flag = jnp.max(over, axis=1, keepdims=True)
+    flag = jnp.where(jnp.max(over, axis=1, keepdims=True) > 0.0, 1.0, 0.0)
     rank = rank.astype(jnp.int32)
     rank0 = rank0.astype(jnp.int32)
     fits = jnp.logical_and(live, rank < CAP)
     fits0 = jnp.logical_and(newest, rank0 < CAP0)
     nowhere = n_src * bd
-    info_ref[0:1, :] = jnp.where(fits, owner * CAP + rank, 0)
+    info_ref[0:1, :] = jnp.clip(jnp.where(fits, owner * CAP + rank, 0), 0, n_obs * CAP - 1)
     info_ref[1:2, :] = jnp.where(live, obs_block, nowhere)
     info_ref[2:3, :] = jnp.where(jnp.logical_and(live, delay > 0), obs_block, nowhere)
     info_ref[3:8, :] = jnp.zeros((5, n_tiles), jnp.int32)
-    key = jnp.where(fits, owner * 128 + rank, FAR)
-    key0 = jnp.where(fits0, owner * 128 + CAP + rank0, FAR)
-    key_d = jnp.where(newest, rank_d.astype(jnp.int32), FAR)
-    code_row = lax.broadcasted_iota(jnp.int32, (16, n_tiles), 0)
-    codes = jnp.zeros((16, n_tiles), jnp.int32)
-    slot0 = jnp.where(fits0, owner * CAP0 + rank0, 0)
-    parts = (
-        place, delay, jnp.bitwise_and(lane, 127), lax.shift_right_logical(lane, 7), slot0,
-        jnp.bitwise_and(obs_block, 127), lax.shift_right_logical(obs_block, 7), jnp.ones_like(lane),
-    )
-    for i, part in enumerate(parts):
-        codes = jnp.where(code_row == i, part, codes)
-    codes = codes.astype(jnp.float32).astype(jnp.bfloat16)
     row = lax.broadcasted_iota(jnp.int32, (128, n_tiles), 0)
-    out_lane = lax.broadcasted_iota(jnp.int32, (1, 128), 1)
-
-    def find(hit):
-        pick = jnp.where(hit, 1.0, 0.0).astype(jnp.bfloat16)
-        return lax.dot_general(codes, pick, (((1,), (1,)), ((), ())), preferred_element_type=jnp.float32)
-
-    def one_owner(o):
-        found = find(jnp.logical_or(key - o * 128 == row, key0 - o * 128 == row))
-        code = found[0:1, :] + found[1:2, :] * bd
-        send_ref[o] = jnp.where(out_lane == 127, flag, code).astype(jnp.int32)
-
-    each(n_obs, one_owner)
-    recv_ref[me] = send_ref[me]
-    entered()
-
-    def send(k):
-        return to_obs(k, n_obs, send_ref.at[lax.rem(me + k, n_obs)], recv_ref.at[me], send_sem, recv_sem)
-
-    each(n_obs, lambda k: send(k).start(), 1)
-    found = find(key_d == row)
-    list_ref[0:1, :] = (found[2:3, :] + found[3:4, :] * 128.0).astype(jnp.int32)
-    list_ref[1:2, :] = found[4:5, :].astype(jnp.int32)
-    list_ref[2:3, :] = jnp.where(found[7:8, :] > 0.5, found[5:6, :] + found[6:7, :] * 128.0, 1.0 * nowhere).astype(jnp.int32)
-    list_ref[3:8, :] = jnp.zeros((5, 128), jnp.int32)
-    each(n_obs, lambda k: send(k).wait(), 1)
+    ones = lambda hit: jnp.where(hit, 1.0, 0.0).astype(jnp.bfloat16)
+    key = jnp.where(fits, rank, FAR)
+    key0 = jnp.where(fits0, rank0 + AT0, FAR)
+    coded = jnp.concatenate([mine * place.astype(jnp.float32), mine * delay.astype(jnp.float32)], axis=0)
+
+    def find(codes, hit):
+        return lax.dot_general(
+            codes.astype(jnp.bfloat16), ones(hit), (((1,), (1,)), ((), ())), preferred_element_type=jnp.float32
+        )
+
+    found = find(coded, jnp.logical_or(key == row, key0 == row))
+    code = found[:n_obs] + found[n_obs:] * bd
+    out_lane = lax.broadcasted_iota(jnp.int32, (n_obs, 128), 1)
+    code = jnp.clip(jnp.where(out_lane == 127, flag, code).astype(jnp.int32), 0, rows - 1)
+    for o in range(n_obs):
+        send_ref[o] = code[o : o + 1]
+
+    def build_list():
+        key_d = jnp.where(newest, rank_d.astype(jnp.int32), FAR)
+        code_row = lax.broadcasted_iota(jnp.int32, (16, n_tiles), 0)
+        codes = jnp.zeros((16, n_tiles), jnp.int32)
+        slot0 = jnp.where(fits0, owner * CAP0 + rank0, 0)
+        parts = (
+            jnp.bitwise_and(lane, 127), lax.shift_right_logical(lane, 7), slot0,
+            jnp.bitwise_and(obs_block, 127), lax.shift_right_logical(obs_block, 7), jnp.ones_like(lane),
+        )
+        for i, part in enumerate(parts):
+            codes = jnp.where(code_row == i, part, codes)
+        found = find(codes.astype(jnp.float32), key_d == row)
+        list_ref[0:1, :] = jnp.clip((found[0:1, :] + found[1:2, :] * 128.0).astype(jnp.int32), 0, n_tiles - 1)
+        list_ref[1:2, :] = jnp.clip(found[2:3, :].astype(jnp.int32), 0, n_obs * CAP0 - 1)
+        block = jnp.where(found[5:6, :] > 0.5, found[3:4, :] + found[4:5, :] * 128.0, 1.0 * nowhere)
+        list_ref[2:3, :] = block.astype(jnp.int32)
+        list_ref[3:8, :] = jnp.zeros((5, 128), jnp.int32)
+
+    return build_list
 
 
 def step_kernel(
-    n_src, n_obs, bd, req, info, lst, info_v, list_v, tiles_ref, hist_ref, inc_ref, near_ref,
-    out_ref, flags_ref,
+    n_src, n_obs, bd, cnt_ref, idx_ref, tiles_ref, hist_ref, inc_ref, near_ref,
+    out_ref, crowded_ref,
+    ask, asked, info_v, list_v, req, info, lst, flags,
     tile, hist, inc, near, rows1, rows2, rows0, send1, send2, send0, mark,
-    y_one, y_high, y_rest, y_new, pick1, pick2, pick0, part_old, part1, part2, recv1, recv2, drive,
-    tile_sem, load_sem, fsend, frecv, send_sem1, recv_sem1, send_sem2, recv_sem2, send_sem0, recv_sem0,
-    rsend1, rrecv1, rsend2, rrecv2,
+    y_one, y_all, y_new, pick1, pick2, pick0, part_old, part1, part2, recv1, recv2, drive,
+    tile_sem, load_sem, ask_send, ask_recv, fsend, frecv, send_sem1, recv_sem1, send_sem2, recv_sem2,
+    send_sem0, recv_sem0, rsend1, rrecv1, rsend2, rrecv2,
 ):
     me_s, me_o = lax.axis_index("src"), lax.axis_index("obs")
     entered = greet(1, 1, n_src, n_obs)
@@ -144,7 +142,6 @@
     chunk = n_tiles // chunks
     width = tiles_ref.shape[2]
     coefs = hist_ref.shape[1]
-    blocks = n_src * bd
     load_hist = pltpu.make_async_copy(hist_ref, hist, load_sem.at[0])
     load_near = pltpu.make_async_copy(near_ref, near, load_sem.at[1])
     load_inc = pltpu.make_async_copy(inc_ref, inc, load_sem.at[2])
@@ -154,22 +151,49 @@
         return pltpu.make_async_copy(tiles_ref.at[at], tile.at[at], tile_sem.at[c])
 
     load_hist.start()
-    flag = req[0, 0, 127]
-    for o in range(1, n_obs):
-        flag = jnp.maximum(flag, req[o, 0, 127])
-    mark[...] = jnp.full(mark.shape, flag, jnp.int32)
-    flags_ref[me_s] = mark[...]
+    build_list = build_requests(n_src, n_obs, bd, hist_ref.shape[0], idx_ref, cnt_ref, ask, info_v, list_v)
+    asked[me_o] = ask[me_o]
+
+    def send_ask(k):
+        return to_obs(k, n_obs, ask.at[lax.rem(me_o + k, n_obs)], asked.at[me_o], ask_send, ask_recv)
+
+    entered()
+    each(n_obs, lambda k: send_ask(k).start(), 1)
+    build_list()
+    info_down = pltpu.make_async_copy(info_v, info, load_sem.at[3])
+    list_down = pltpu.make_async_copy(list_v, lst, load_sem.at[4])
+    info_down.start()
+    list_down.start()
+    ones = lambda hit: jnp.where(hit, 1.0, 0.0).astype(jnp.bfloat16)
+    row = lax.broadcasted_iota(jnp.int32, (bd, n_tiles), 0)
+    row0 = lax.broadcasted_iota(jnp.int32, (bd, CAPD), 0)
+
+    def one_pick(k):
+        first = lax.rem(me_s + k + 1, n_src) * bd
+        at = pl.ds(pl.multiple_of(k * bd, bd), bd)
+        pick1[at, :] = ones(info_v[1:2, :] - first == row)
+        pick2[at, :] = ones(info_v[2:3, :] - first == row)
+        pick0[at, :] = ones(list_v[2:3, 0:CAPD] - first == row0)
+
+    each(n_src, one_pick)
+    each(n_obs, lambda k: send_ask(k).wait(), 1)
+    req_down = pltpu.make_async_copy(asked, req, load_sem.at[5])
+    req_down.start()
+    worst = jnp.max(asked[...].astype(jnp.float32), axis=0)
+    worst = jnp.where(lax.broadcasted_iota(jnp.int32, worst.shape, 1) == 127, worst, 0.0)
+    mark[...] = jnp.broadcast_to(jnp.max(worst, axis=1, keepdims=True), mark.shape)
+    flags[me_s] = mark[...]
 
     def gather(table, out, o, slots, first, code_to_row):
-        def eight(turn):
-            for i in range(8):
-                r = turn * 8 + i
+        def twelve(turn):
+            for i in range(12):
+                r = turn * 12 + i
                 out[r] = table[code_to_row(req[o, 0, first + r])]
 
-        each(slots // 8, eight)
+        each(slots // 12, twelve)
 
     def send_flag(k):
-        return to_src(k, n_src, mark, flags_ref.at[me_s], fsend, frecv)
+        return to_src(k, n_src, mark, flags.at[me_s], fsend, frecv)
 
     def send_rows(k, send, rows, cap, send_sem, recv_sem):
         return to_obs(k, n_obs, send.at[k], rows.at[pl.ds(me_o * cap, cap)], send_sem, recv_sem)
@@ -181,36 +205,22 @@
         return send_rows(k, send1, rows1, CAP, send_sem1, recv_sem1)
 
     load_hist.wait()
-    one_dest(1)
-    load_inc.start()
-    load_near.start()
-    each(chunks, lambda c: load_tiles(c).start())
-    entered()
-    send_one(1).start()
+    req_down.wait()
 
     def gather_send(k):
         one_dest(k)
         send_one(k).start()
 
-    each(n_obs, gather_send, 2)
+    each(n_obs, gather_send, 1)
+    each(chunks, lambda c: load_tiles(c).start())
+    load_inc.start()
+    load_near.start()
     each(n_src, lambda k: send_flag(k).start(), 1)
     gather(hist, rows1.at[pl.ds(me_o * CAP, CAP)], me_o, CAP, 0, lambda c: c)
 
     older = lambda c: jnp.maximum(c - bd, 0)
     each(n_obs, lambda k: gather(hist, send2.at[k], lax.rem(me_o + k, n_obs), CAP, 0, older), 1)
     gather(hist, rows2.at[pl.ds(me_o * CAP, CAP)], me_o, CAP, 0, older)
-
-    row = lax.broadcasted_iota(jnp.int32, (bd, n_tiles), 0)
-    row0 = lax.broadcasted_iota(jnp.int32, (bd, CAPD), 0)
-
-    def one_pick(j):
-        at = pl.ds(j * bd, bd)
-        ones = lambda hit: jnp.where(hit, 1.0, 0.0).astype(jnp.bfloat16)
-        pick1[j] = ones(info_v[1:2, :] - j * bd == row)
-        pick2[j] = ones(info_v[2:3, :] - j * bd == row)
-        pick0[j] = ones(list_v[2:3, 0:CAPD] - j * bd == row0)
-
-    each(n_src, one_pick)
 
     def two_products(x0, x1, t0, t1, y, count, at):
         x = jnp.concatenate([x0.astype(jnp.float32), x1.astype(jnp.float32)], axis=0).astype(jnp.bfloat16)
@@ -226,29 +236,24 @@
 
         return one_chunk
 
-    def split():
+    def pack():
         for c in range(coefs):
             lanes = slice(c * width, (c + 1) * width)
 
             def some(i):
                 at = pl.multiple_of(i * 64, 64)
-                value = y_one[pl.ds(c * n_tiles + at, 64), :]
-                high = value.astype(jnp.bfloat16)
-                y_high[pl.ds(at, 64), lanes] = high
-                y_rest[pl.ds(at, 64), lanes] = (value - high.astype(jnp.float32)).astype(jnp.bfloat16)
+                y_all[pl.ds(at, 64), lanes] = y_one[pl.ds(c * n_tiles + at, 64), :].astype(jnp.bfloat16)
 
             each(n_tiles // 64, some)
 
-    def add_up(pick):
-        return jnp.dot(pick, y_high[...], preferred_element_type=jnp.float32) + jnp.dot(
-            pick, y_rest[...], preferred_element_type=jnp.float32
-        )
-
     def send_part(k, part, recv, send_sem, recv_sem):
-        return to_src(k, n_src, part.at[lax.rem(me_s + k, n_src)], recv.at[me_s], send_sem, recv_sem)
+        return to_src(k, n_src, part.at[pl.ds((k - 1) * bd, bd)], recv.at[me_s], send_sem, recv_sem)
+
+    group = n_src // 2
+    half = lambda g: slice(g * group * bd, (g + 1) * group * bd)
 
     def solve(which, recv, part):
-        total = part[me_s].astype(jnp.float32)
+        total = part[(n_src - 1) * bd :, :].astype(jnp.float32)
         for k in range(1, n_src):
             total = total + recv[lax.rem(me_s + k, n_src)].astype(jnp.float32)
         for c in range(coefs):
@@ -270,22 +275,21 @@
 
     send_two = lambda k: send_rows(k, send2, rows2, CAP, send_sem2, recv_sem2)
     each(chunks, lambda c: load_tiles(c).wait())
+    info_down.wait()
     each(n_obs, lambda k: send_one(k).wait(), 1)
     each(n_obs, lambda k: send_two(k).start(), 1)
     each(chunks, products(rows1))
-    split()
+    pack()
     part_one = lambda k: send_part(k, part1, recv1, rsend1, rrecv1)
-
-    def sum_send_one(k):
-        j = lax.rem(me_s + k, n_src)
-        part1[j] = add_up(pick1[j]).astype(jnp.bfloat16)
-        part_one(k).start()
-
-    each(n_src, sum_send_one, 1)
-    part1[me_s] = add_up(pick1[me_s]).astype(jnp.bfloat16)
+    for g in range(2):
+        part1[half(g), :] = jnp.dot(
+            pick1[half(g), :], y_all[...], preferred_element_type=jnp.float32
+        ).astype(jnp.bfloat16)
+        each(min(group * (g + 1) + 1, n_src), lambda k: part_one(k).start(), group * g + 1)
     load_inc.wait()
     load_near.wait()
     each(n_src, lambda k: part_one(k).wait(), 1)
+    each(n_src, lambda k: send_flag(k).wait(), 1)
     solve(0, recv1, part1)
 
     newest = out_ref.at[0]
@@ -293,19 +297,17 @@
     send_new = lambda k: send_rows(k, send0, rows0, CAP0, send_sem0, recv_sem0)
 
     def gather_send_new(k):
-        gather(newest, send0.at[k], lax.rem(me_o + k, n_obs), CAP0, CAP, placed)
+        gather(newest, send0.at[k], lax.rem(me_o + k, n_obs), CAP0, AT0, placed)
         send_new(k).start()
 
     each(n_obs, gather_send_new, 1)
-    gather(newest, rows0.at[pl.ds(me_o * CAP0, CAP0)], me_o, CAP0, CAP, placed)
+    gather(newest, rows0.at[pl.ds(me_o * CAP0, CAP0)], me_o, CAP0, AT0, placed)
     each(n_obs, lambda k: send_two(k).wait(), 1)
     each(chunks, products(rows2))
-    split()
-
-    def sum_old(j):
-        part_old[j] = add_up(pick2[j])
-
-    each(n_src, sum_old)
+    pack()
+    for g in range(2):
+        part_old[half(g), :] = jnp.dot(pick2[half(g), :], y_all[...], preferred_element_type=jnp.float32)
+    list_down.wait()
     each(n_obs, lambda k: send_new(k).wait(), 1)
 
     def new_products(turn):
@@ -317,25 +319,15 @@
 
     each(CAPD // 8, new_products)
     value = jnp.concatenate([y_new[c * CAPD : (c + 1) * CAPD, :] for c in range(coefs)], axis=1)
-    high = value.astype(jnp.bfloat16)
-    rest = (value - high.astype(jnp.float32)).astype(jnp.bfloat16)
+    value = value.astype(jnp.bfloat16)
     part_two = lambda k: send_part(k, part2, recv2, rsend2, rrecv2)
-
-    def sum_two(j):
-        added = jnp.dot(pick0[j], high, preferred_element_type=jnp.float32) + jnp.dot(
-            pick0[j], rest, preferred_element_type=jnp.float32
-        )
-        part2[j] = (part_old[j] + added).astype(jnp.bfloat16)
-
-    def sum_send_two(k):
-        sum_two(lax.rem(me_s + k, n_src))
-        part_two(k).start()
-
-    each(n_src, sum_send_two, 1)
-    sum_two(me_s)
+    for g in range(2):
+        added = jnp.dot(pick0[half(g), :], value, preferred_element_type=jnp.float32)
+        part2[half(g), :] = (part_old[half(g), :] + added).astype(jnp.bfloat16)
+        each(min(group * (g + 1) + 1, n_src), lambda k: part_two(k).start(), group * g + 1)
     each(n_src, lambda k: part_two(k).wait(), 1)
     solve(1, recv2, part2)
-    each(n_src, lambda k: send_flag(k).wait(), 1)
+    crowded_ref[0, 0] = jnp.max(flags[...])
 
 
 def dense_path(tile_rows, index_rows, live_count, history, incident, near_inverse, n_src, n_obs):
@@ -409,7 +401,7 @@
     n_src, n_obs = mesh.shape["src"], mesh.shape["obs"]
     vmem = pl.BlockSpec(memory_space=pltpu.VMEM)
     smem = pl.BlockSpec(memory_space=pltpu.SMEM)
-    anywhere = pl.BlockSpec(memory_space=pl.ANY)
+    hbm = pl.BlockSpec(memory_space=pltpu.HBM)
     dma = pltpu.SemaphoreType.DMA
     f32, bf16, i32 = jnp.float32, jnp.bfloat16, jnp.int32
 
@@ -425,20 +417,6 @@
         hist = history.reshape(slots, coefs, bd, width).transpose(0, 2, 1, 3).reshape(slots * bd, coefs, width)
         drive = incident.reshape(2, coefs, bd, width).transpose(0, 2, 1, 3)
 
-        requests, info, newest = pl.pallas_call(
-            functools.partial(request_kernel, n_src, n_obs, bd),
-            name="requests",
-            out_shape=(
-                jax.ShapeDtypeStruct((n_obs, 1, 128), i32),
-                jax.ShapeDtypeStruct((8, n_tiles), i32),
-                jax.ShapeDtypeStruct((8, 128), i32),
-            ),
-            in_specs=[vmem, smem],
-            out_specs=(vmem, vmem, vmem),
-            scratch_shapes=[pltpu.VMEM((n_obs, 1, 128), i32), dma((n_obs,)), dma((n_obs,))],
-            compiler_params=params(0),
-        )(index_rows, tile_count)
-
         def rows(cap):
             return pltpu.VMEM((n_obs * cap, coefs, width), bf16)
 
@@ -446,45 +424,49 @@
             return pltpu.VMEM((n_obs, cap, coefs, width), bf16)
 
         def parts(kind):
-            return pltpu.VMEM((n_src, bd, coefs * width), kind)
+            return pltpu.VMEM((n_src * bd, coefs * width), kind)
+
+        arrived = pltpu.VMEM((n_src, bd, coefs * width), bf16)
 
         chunks = max(1, n_tiles // 32)
-        both, flags = pl.pallas_call(
+        both, crowded = pl.pallas_call(
             functools.partial(step_kernel, n_src, n_obs, bd),
             name="step",
             out_shape=(
                 jax.ShapeDtypeStruct((2, bd, coefs, width), bf16),
-                jax.ShapeDtypeStruct((n_src, 1, 128), i32),
+                jax.ShapeDtypeStruct((1, 1), f32),
             ),
-            in_specs=[smem, smem, smem, vmem, vmem, anywhere, anywhere, anywhere, anywhere],
-            out_specs=(vmem, vmem),
+            in_specs=[smem, vmem, hbm, hbm, hbm, hbm],
+            out_specs=(vmem, smem),
             scratch_shapes=[
+                pltpu.VMEM((n_obs, 1, 128), i32), pltpu.VMEM((n_obs, 1, 128), i32),
+                pltpu.VMEM((8, n_tiles), i32), pltpu.VMEM((8, 128), i32),
+                pltpu.SMEM((n_obs, 1, 128), i32), pltpu.SMEM((8, n_tiles), i32), pltpu.SMEM((8, 128), i32),
+                pltpu.VMEM((n_src, 1, 128), f32),
                 pltpu.VMEM((n_tiles, width, width), bf16),
                 pltpu.VMEM(hist.shape, bf16),
                 pltpu.VMEM(drive.shape, f32),
                 pltpu.VMEM((bd, width, width), bf16),
                 rows(CAP), rows(CAP), rows(CAP0), sends(CAP), sends(CAP), sends(CAP0),
-                pltpu.VMEM((1, 128), i32),
+                pltpu.VMEM((1, 128), f32),
                 pltpu.VMEM((coefs * n_tiles, width), f32),
                 pltpu.VMEM((n_tiles, coefs * width), bf16),
-                pltpu.VMEM((n_tiles, coefs * width), bf16),
                 pltpu.VMEM((coefs * CAPD, width), f32),
-                pltpu.VMEM((n_src, bd, n_tiles), bf16),
-                pltpu.VMEM((n_src, bd, n_tiles), bf16),
-                pltpu.VMEM((n_src, bd, CAPD), bf16),
-                parts(f32), parts(bf16), parts(bf16), parts(bf16), parts(bf16),
+                pltpu.VMEM((n_src * bd, n_tiles), bf16),
+                pltpu.VMEM((n_src * bd, n_tiles), bf16),
+                pltpu.VMEM((n_src * bd, CAPD), bf16),
+                parts(f32), parts(bf16), parts(bf16), arrived, arrived,
                 pltpu.VMEM((coefs * bd, width), f32),
-                dma((chunks,)), dma((3,)),
+                dma((chunks,)), dma((6,)), dma((n_obs,)), dma((n_obs,)),
                 dma((n_src,)), dma((n_src,)),
                 dma((n_obs,)), dma((n_obs,)), dma((n_obs,)), dma((n_obs,)), dma((n_obs,)), dma((n_obs,)),
                 dma((n_src,)), dma((n_src,)), dma((n_src,)), dma((n_src,)),
             ],
-            compiler_params=params(1),
-        )(requests, info, newest, info, newest, tile_rows, hist, drive, near_inverse)
-        crowded = jnp.max(flags) > 0
+            compiler_params=params(0),
+        )(tile_count, index_rows, tile_rows, hist, drive, near_inverse)
 
         both = lax.cond(
-            crowded,
+            crowded[0, 0] > 0.0,
             lambda kept: dense_path(
                 tile_rows, tile_index.reshape(3, n_tiles), tile_count.reshape(()), history, drive, near_inverse,
                 n_src, n_obs,

time: 80 us -> 70.1 us (0.88)
  Pallas kernels: 75.1 us -> 65.8 us
  other arithmetic: 1.32 us -> 0 us
    pallas_call x1 -> x0, Pallas kernels: 11.6 us -> none  [on_device(): pl.pallas_call(functools.partial(request_kernel, n_src, n_obs, bd), name=...]
    pallas_call x1, Pallas kernels: 63.5 us -> 65.8 us  [on_device(): pl.pallas_call(functools.partial(step_kernel, n_src, n_obs, bd), name='st...]
    reduce_max x1 -> x0, other arithmetic: 1.32 us -> none  [on_device(): crowded = jnp.max(flags) > 0]
where the time goes in v4:
time: 70.1 us; the launch traced here: 69.1 us
  Pallas kernels  65.8 us (94%)
  local copies, waits for them, and re-layouts  1.93 us (3%)
  between operations  1.31 us (2%)
    pallas_call x1, Pallas kernels, on_device(): pl.pallas_call(functools.partial(step_kernel, n_src, n_obs, bd), name='st...  65.8 us
    unnamed x6, local copies, waits for them, and re-layouts  1.93 us

profile of v4, /device:TPU:1, one launch (start us, length us, event | category | flops | bytes accessed | tf_op | source)
XLA Modules:
  0.0 69.1 jit_solution(17980052927895884529)
XLA Ops:
  0.0 0.0 copy-start.1
  0.0 0.0 copy-start
  0.0 1.3 %copy.71 = bf16[16,4,8192]{2,1,0:T(4,128)(2,1)S(1)} copy(bf16[16,4,8192]{2,1,0:T(4,128)(2,1)} %param.23) | data formatting | bytes 2097152
  1.9 65.8 %step.1 = (bf16[2,64,4,128]{3,2,1,0:T(4,128)(2,1)S(1)}, f32[1,1]{1,0:T(1,128)}) custom-call(s32[1,1]{1,0:T(1,128)S(6)} %copy.69.cnt_ref, s32[3,1,512]{2,1,0:T(1,128)} %bitcast.127, bf16[512,128,128]{2,1,0:T(8,128)(2,1)} %bitcast.118, bf16[1024,4,128]{2,1,0:T(4,128)(2,1)S(1)} %bitcast.120, f32[2,64,4,128]{3,2,1,0:T(4,128)} %bitcast.122, ...), custom_call_target="tpu_custom_call" | custom-call | tf_op jit(solution)/shard_map/step/pallas_call | solution.py:432
  68.4 0.0 copy-done.1
  68.4 0.0 copy-done
  68.4 0.7 copy.72
  (1 shorter events, 0.0 us)
Async XLA Ops:
  0.0 68.4 %copy-start.1 = (s32[1,1,3,512]{3,1,2,0:T(1,128)S(1)}, s32[1,1,3,512]{3,1,2,0:T(1,128)}, u32[]{:S(2)}) copy-start(s32[1,1,3,512]{3,1,2,0:T(1,128)} %param.21) | copy-start | bytes 18436
  0.0 68.4 %copy-start = (f32[2,4,8192]{2,1,0:T(4,128)S(1)}, f32[2,4,8192]{2,1,0:T(4,128)}, u32[]{:S(2)}) copy-start(f32[2,4,8192]{2,1,0:T(4,128)} %param.24) | copy-start | bytes 786436

commit v5 on v4

--- a/solution.py
+++ b/solution.py
@@ -12,6 +12,8 @@
 CAP0 = 12
 CAPD = 64
 FAR = -(1 << 20)
+ORDER = (10, 11, 8, 9, 6, 14, 7, 15, 4, 12, 5, 13, 2, 3, 1)
+STAGED = (False, False)
 AT0 = 64
 
 
@@ -26,26 +28,36 @@
     if obs_peers:
         for k in range(1, n_obs):
             pl.semaphore_signal(
-                barrier, inc=1, device_id=(me_s, lax.rem(me_o + k, n_obs)), device_id_type=MESH
+                barrier, inc=1, device_id=(me_s, obs_peer(k, n_obs)), device_id_type=MESH
             )
     total = (n_src - 1) * src_peers + (n_obs - 1) * obs_peers
     return lambda: pl.semaphore_wait(barrier, total)
 
 
+def obs_peer(k, n_obs):
+    me = lax.axis_index("obs")
+    x = lax.rem(me // 4 + k // 4, n_obs // 4)
+    z = lax.rem(lax.rem(me // 2, 2) + lax.rem(k // 2, 2), 2)
+    core = lax.rem(lax.rem(me, 2) + lax.rem(k, 2), 2)
+    return x * 4 + z * 2 + core
+
+
 def to_obs(k, n_obs, src_ref, dst_ref, send_sem, recv_sem):
-    me_s, me_o = lax.axis_index("src"), lax.axis_index("obs")
     return pltpu.make_async_remote_copy(
-        src_ref=src_ref, dst_ref=dst_ref, send_sem=send_sem.at[k], recv_sem=recv_sem.at[k],
-        device_id=(me_s, lax.rem(me_o + k, n_obs)), device_id_type=MESH,
+        src_ref=src_ref, dst_ref=dst_ref, send_sem=send_sem, recv_sem=recv_sem,
+        device_id=(lax.axis_index("src"), obs_peer(k, n_obs)), device_id_type=MESH,
     )
 
 
-def to_src(k, n_src, src_ref, dst_ref, send_sem, recv_sem):
-    me_s, me_o = lax.axis_index("src"), lax.axis_index("obs")
+def to_src(peer, src_ref, dst_ref, send_sem, recv_sem):
     return pltpu.make_async_remote_copy(
-        src_ref=src_ref, dst_ref=dst_ref, send_sem=send_sem.at[k], recv_sem=recv_sem.at[k],
-        device_id=(lax.rem(me_s + k, n_src), me_o), device_id_type=MESH,
+        src_ref=src_ref, dst_ref=dst_ref, send_sem=send_sem, recv_sem=recv_sem,
+        device_id=(peer, lax.axis_index("obs")), device_id_type=MESH,
     )
+
+
+def take(ref, sem):
+    pltpu.make_async_copy(ref, ref, sem).wait()
 
 
 def each(count, body, start=0):
@@ -56,7 +68,7 @@
     n_tiles = idx_ref.shape[2]
     shift = bd.bit_length() - 1
     lane = lax.broadcasted_iota(jnp.int32, (1, n_tiles), 1)
-    live = lane < cnt_ref[0, 0]
+    live = lane < cnt_ref[...]
     obs_block, source, delay = idx_ref[0], idx_ref[1], idx_ref[2]
     owner = lax.shift_right_logical(source, shift)
     place = jnp.bitwise_and(source, bd - 1)
@@ -131,15 +143,15 @@
     out_ref, crowded_ref,
     ask, asked, info_v, list_v, req, info, lst, flags,
     tile, hist, inc, near, rows1, rows2, rows0, send1, send2, send0, mark,
-    y_one, y_all, y_new, pick1, pick2, pick0, part_old, part1, part2, recv1, recv2, drive,
-    tile_sem, load_sem, ask_send, ask_recv, fsend, frecv, send_sem1, recv_sem1, send_sem2, recv_sem2,
-    send_sem0, recv_sem0, rsend1, rrecv1, rsend2, rrecv2,
+    y_one, y_all, y_new, pick1, pick2, pick0, part_old, part1, part2, recv1, recv2, far_out, far_in, drive,
+    tile_sem, load_sem, ask_sem, flag_sem, sem1, sem2, sem0, part_sem1, part_sem2, far_sem1, far_sem2,
 ):
     me_s, me_o = lax.axis_index("src"), lax.axis_index("obs")
+    order = ORDER if n_obs == len(ORDER) + 1 else range(1, n_obs)
     entered = greet(1, 1, n_src, n_obs)
     n_tiles = tiles_ref.shape[0]
-    chunks = tile_sem.shape[0]
-    chunk = n_tiles // chunks
+    chunk = min(32, n_tiles)
+    chunks = n_tiles // chunk
     width = tiles_ref.shape[2]
     coefs = hist_ref.shape[1]
     load_hist = pltpu.make_async_copy(hist_ref, hist, load_sem.at[0])
@@ -148,14 +160,14 @@
 
     def load_tiles(c):
         at = pl.ds(c * chunk, chunk)
-        return pltpu.make_async_copy(tiles_ref.at[at], tile.at[at], tile_sem.at[c])
+        return pltpu.make_async_copy(tiles_ref.at[at], tile.at[at], tile_sem)
 
     load_hist.start()
     build_list = build_requests(n_src, n_obs, bd, hist_ref.shape[0], idx_ref, cnt_ref, ask, info_v, list_v)
     asked[me_o] = ask[me_o]
 
     def send_ask(k):
-        return to_obs(k, n_obs, ask.at[lax.rem(me_o + k, n_obs)], asked.at[me_o], ask_send, ask_recv)
+        return to_obs(k, n_obs, ask.at[obs_peer(k, n_obs)], asked.at[me_o], ask_sem.at[0], ask_sem.at[1])
 
     entered()
     each(n_obs, lambda k: send_ask(k).start(), 1)
@@ -168,15 +180,23 @@
     row = lax.broadcasted_iota(jnp.int32, (bd, n_tiles), 0)
     row0 = lax.broadcasted_iota(jnp.int32, (bd, CAPD), 0)
 
+    n_y = n_src // 2
+    me_z, me_y = me_s // n_y, lax.rem(me_s, n_y)
+
+    def place_of(k):
+        return lax.rem(me_z + 1 - k // n_y, 2) * n_y + lax.rem(me_y + 1 + lax.rem(k, n_y), n_y)
+
     def one_pick(k):
-        first = lax.rem(me_s + k + 1, n_src) * bd
+        first = place_of(k) * bd
         at = pl.ds(pl.multiple_of(k * bd, bd), bd)
         pick1[at, :] = ones(info_v[1:2, :] - first == row)
         pick2[at, :] = ones(info_v[2:3, :] - first == row)
         pick0[at, :] = ones(list_v[2:3, 0:CAPD] - first == row0)
 
     each(n_src, one_pick)
-    each(n_obs, lambda k: send_ask(k).wait(), 1)
+    others = pl.ds(0, n_obs - 1)
+    take(asked.at[others], ask_sem.at[1])
+    take(ask.at[others], ask_sem.at[0])
     req_down = pltpu.make_async_copy(asked, req, load_sem.at[5])
     req_down.start()
     worst = jnp.max(asked[...].astype(jnp.float32), axis=0)
@@ -193,16 +213,20 @@
         each(slots // 12, twelve)
 
     def send_flag(k):
-        return to_src(k, n_src, mark, flags.at[me_s], fsend, frecv)
-
-    def send_rows(k, send, rows, cap, send_sem, recv_sem):
-        return to_obs(k, n_obs, send.at[k], rows.at[pl.ds(me_o * cap, cap)], send_sem, recv_sem)
+        return to_src(lax.rem(me_s + k, n_src), mark, flags.at[me_s], flag_sem.at[0], flag_sem.at[1])
+
+    def send_rows(k, send, rows, cap, sem):
+        return to_obs(k, n_obs, send.at[k], rows.at[pl.ds(me_o * cap, cap)], sem.at[0], sem.at[1])
+
+    def take_rows(send, rows, cap, sem):
+        take(rows.at[pl.ds(0, (n_obs - 1) * cap)], sem.at[1])
+        take(send.at[pl.ds(1, n_obs - 1)], sem.at[0])
 
     def one_dest(k):
-        gather(hist, send1.at[k], lax.rem(me_o + k, n_obs), CAP, 0, lambda c: c)
+        gather(hist, send1.at[k], obs_peer(k, n_obs), CAP, 0, lambda c: c)
 
     def send_one(k):
-        return send_rows(k, send1, rows1, CAP, send_sem1, recv_sem1)
+        return send_rows(k, send1, rows1, CAP, sem1)
 
     load_hist.wait()
     req_down.wait()
@@ -211,7 +235,8 @@
         one_dest(k)
         send_one(k).start()
 
-    each(n_obs, gather_send, 1)
+    for k in order:
+        gather_send(k)
     each(chunks, lambda c: load_tiles(c).start())
     load_inc.start()
     load_near.start()
@@ -219,7 +244,12 @@
     gather(hist, rows1.at[pl.ds(me_o * CAP, CAP)], me_o, CAP, 0, lambda c: c)
 
     older = lambda c: jnp.maximum(c - bd, 0)
-    each(n_obs, lambda k: gather(hist, send2.at[k], lax.rem(me_o + k, n_obs), CAP, 0, older), 1)
+    def gather_send_two(k):
+        gather(hist, send2.at[k], obs_peer(k, n_obs), CAP, 0, older)
+        send_rows(k, send2, rows2, CAP, sem2).start()
+
+    for k in order:
+        gather_send_two(k)
     gather(hist, rows2.at[pl.ds(me_o * CAP, CAP)], me_o, CAP, 0, older)
 
     def two_products(x0, x1, t0, t1, y, count, at):
@@ -246,16 +276,43 @@
 
             each(n_tiles // 64, some)
 
-    def send_part(k, part, recv, send_sem, recv_sem):
-        return to_src(k, n_src, part.at[pl.ds((k - 1) * bd, bd)], recv.at[me_s], send_sem, recv_sem)
+    def start_half(g, staged, part, recv, sem):
+        for i in range(n_y - staged if g == 0 else n_y - 1):
+            k = g * n_y + i
+            peer = me_z * n_y + lax.rem(me_y + 1 + i, n_y) if staged else place_of(k)
+            to_src(peer, part.at[pl.ds(k * bd, bd)], recv.at[k], sem.at[0], sem.at[1 + g]).start()
+
+    def finish(staged, part, recv, sem, far_sem):
+        def half_sum(g, count):
+            if count:
+                take(recv.at[pl.ds(g * n_y, count)], sem.at[1 + g])
+            total = part[(g * n_y + n_y - 1) * bd : (g + 1) * n_y * bd, :].astype(jnp.float32)
+            for i in range(n_y - 1):
+                total = total + recv[g * n_y + i].astype(jnp.float32)
+            return total
+
+        sent = n_src - 2 if staged else n_src - 1
+        if staged:
+            far_out[...] = half_sum(0, n_y - 1).astype(jnp.bfloat16)
+            peer = lax.rem(me_z + 1, 2) * n_y + me_y
+            far = to_src(peer, far_out, far_in, far_sem.at[0], far_sem.at[1])
+            far.start()
+            total = half_sum(1, n_y - 1)
+            far.wait()
+            total = total + far_in[...].astype(jnp.float32)
+        else:
+            take(recv.at[pl.ds(0, n_y)], sem.at[1])
+            total = half_sum(1, n_y - 1)
+            for k in range(n_y):
+                total = total + recv[k].astype(jnp.float32)
+        if sent:
+            take(recv.at[pl.ds(0, sent)], sem.at[0])
+        return total
 
     group = n_src // 2
     half = lambda g: slice(g * group * bd, (g + 1) * group * bd)
 
-    def solve(which, recv, part):
-        total = part[(n_src - 1) * bd :, :].astype(jnp.float32)
-        for k in range(1, n_src):
-            total = total + recv[lax.rem(me_s + k, n_src)].astype(jnp.float32)
+    def solve(which, total):
         for c in range(coefs):
             drive[pl.ds(c * bd, bd), :] = total[:, c * width : (c + 1) * width]
 
@@ -273,42 +330,39 @@
 
         each(bd // 8, pairs)
 
-    send_two = lambda k: send_rows(k, send2, rows2, CAP, send_sem2, recv_sem2)
-    each(chunks, lambda c: load_tiles(c).wait())
+    take(tile, tile_sem)
     info_down.wait()
-    each(n_obs, lambda k: send_one(k).wait(), 1)
-    each(n_obs, lambda k: send_two(k).start(), 1)
+    take_rows(send1, rows1, CAP, sem1)
     each(chunks, products(rows1))
     pack()
-    part_one = lambda k: send_part(k, part1, recv1, rsend1, rrecv1)
     for g in range(2):
         part1[half(g), :] = jnp.dot(
             pick1[half(g), :], y_all[...], preferred_element_type=jnp.float32
         ).astype(jnp.bfloat16)
-        each(min(group * (g + 1) + 1, n_src), lambda k: part_one(k).start(), group * g + 1)
+        start_half(g, STAGED[0], part1, recv1, part_sem1)
     load_inc.wait()
     load_near.wait()
-    each(n_src, lambda k: part_one(k).wait(), 1)
-    each(n_src, lambda k: send_flag(k).wait(), 1)
-    solve(0, recv1, part1)
+    for side in range(2):
+        take(flags.at[pl.ds(0, n_src - 1)], flag_sem.at[side])
+    solve(0, finish(STAGED[0], part1, recv1, part_sem1, far_sem1))
 
     newest = out_ref.at[0]
     placed = lambda c: jnp.bitwise_and(c, bd - 1)
-    send_new = lambda k: send_rows(k, send0, rows0, CAP0, send_sem0, recv_sem0)
+    send_new = lambda k: send_rows(k, send0, rows0, CAP0, sem0)
 
     def gather_send_new(k):
-        gather(newest, send0.at[k], lax.rem(me_o + k, n_obs), CAP0, AT0, placed)
+        gather(newest, send0.at[k], obs_peer(k, n_obs), CAP0, AT0, placed)
         send_new(k).start()
 
     each(n_obs, gather_send_new, 1)
     gather(newest, rows0.at[pl.ds(me_o * CAP0, CAP0)], me_o, CAP0, AT0, placed)
-    each(n_obs, lambda k: send_two(k).wait(), 1)
+    take_rows(send2, rows2, CAP, sem2)
     each(chunks, products(rows2))
     pack()
     for g in range(2):
         part_old[half(g), :] = jnp.dot(pick2[half(g), :], y_all[...], preferred_element_type=jnp.float32)
     list_down.wait()
-    each(n_obs, lambda k: send_new(k).wait(), 1)
+    take_rows(send0, rows0, CAP0, sem0)
 
     def new_products(turn):
         for i in range(0, 8, 2):
@@ -320,13 +374,11 @@
     each(CAPD // 8, new_products)
     value = jnp.concatenate([y_new[c * CAPD : (c + 1) * CAPD, :] for c in range(coefs)], axis=1)
     value = value.astype(jnp.bfloat16)
-    part_two = lambda k: send_part(k, part2, recv2, rsend2, rrecv2)
     for g in range(2):
         added = jnp.dot(pick0[half(g), :], value, preferred_element_type=jnp.float32)
         part2[half(g), :] = (part_old[half(g), :] + added).astype(jnp.bfloat16)
-        each(min(group * (g + 1) + 1, n_src), lambda k: part_two(k).start(), group * g + 1)
-    each(n_src, lambda k: part_two(k).wait(), 1)
-    solve(1, recv2, part2)
+        start_half(g, STAGED[1], part2, recv2, part_sem2)
+    solve(1, finish(STAGED[1], part2, recv2, part_sem2, far_sem2))
     crowded_ref[0, 0] = jnp.max(flags[...])
 
 
@@ -340,13 +392,14 @@
         ring = [(i, (i + 1) % n_obs) for i in range(n_obs)]
         me = lax.axis_index("obs")
         whole = jnp.zeros((n_obs,) + block.shape, block.dtype)
+        whole = lax.dynamic_update_index_in_dim(whole, block, me, 0)
 
         def hop(k, carry):
             whole, moving = carry
             whole = lax.dynamic_update_index_in_dim(whole, moving, lax.rem(me - k + n_obs, n_obs), 0)
             return whole, lax.ppermute(moving, "obs", ring)
 
-        return lax.fori_loop(0, n_obs, hop, (whole, block))[0]
+        return lax.fori_loop(1, n_obs, hop, (whole, lax.ppermute(block, "obs", ring)))[0]
 
     def sum_src(value):
         ring = [(i, (i + 1) % n_src) for i in range(n_src)]
@@ -428,7 +481,6 @@
 
         arrived = pltpu.VMEM((n_src, bd, coefs * width), bf16)
 
-        chunks = max(1, n_tiles // 32)
         both, crowded = pl.pallas_call(
             functools.partial(step_kernel, n_src, n_obs, bd),
             name="step",
@@ -436,7 +488,7 @@
                 jax.ShapeDtypeStruct((2, bd, coefs, width), bf16),
                 jax.ShapeDtypeStruct((1, 1), f32),
             ),
-            in_specs=[smem, vmem, hbm, hbm, hbm, hbm],
+            in_specs=[vmem, vmem, hbm, hbm, hbm, hbm],
             out_specs=(vmem, smem),
             scratch_shapes=[
                 pltpu.VMEM((n_obs, 1, 128), i32), pltpu.VMEM((n_obs, 1, 128), i32),
@@ -456,11 +508,9 @@
                 pltpu.VMEM((n_src * bd, n_tiles), bf16),
                 pltpu.VMEM((n_src * bd, CAPD), bf16),
                 parts(f32), parts(bf16), parts(bf16), arrived, arrived,
+                pltpu.VMEM((bd, coefs * width), bf16), pltpu.VMEM((bd, coefs * width), bf16),
                 pltpu.VMEM((coefs * bd, width), f32),
-                dma((chunks,)), dma((6,)), dma((n_obs,)), dma((n_obs,)),
-                dma((n_src,)), dma((n_src,)),
-                dma((n_obs,)), dma((n_obs,)), dma((n_obs,)), dma((n_obs,)), dma((n_obs,)), dma((n_obs,)),
-                dma((n_src,)), dma((n_src,)), dma((n_src,)), dma((n_src,)),
+                dma, dma((6,)), dma((2,)), dma((2,)), dma((2,)), dma((2,)), dma((2,)), dma((3,)), dma((3,)), dma((2,)), dma((2,)),
             ],
             compiler_params=params(0),
         )(tile_count, index_rows, tile_rows, hist, drive, near_inverse)

time: 70.1 us -> 66.4 us (0.947); the launches traced: 69.1 us -> 66.2 us
  Pallas kernels: 65.8 us -> 63.9 us
  local copies, waits for them, and re-layouts: 1.93 us -> 0.67 us
    pallas_call x1, Pallas kernels: 65.8 us -> 63.9 us  [on_device(): pl.pallas_call(functools.partial(step_kernel, n_src, n_obs, bd), name='st...]
    unnamed x6 -> x7, local copies, waits for them, and re-layouts: 1.93 us -> 0.67 us
where the time goes in v5:
time: 66.4 us; the launch traced here: 66.2 us
  Pallas kernels  63.9 us (96%)
  between operations  1.43 us (2%)
  local copies, waits for them, and re-layouts  0.67 us (1%)
    pallas_call x1, Pallas kernels, on_device(): pl.pallas_call(functools.partial(step_kernel, n_src, n_obs, bd), name='st...  63.9 us

profile of v5, /device:TPU:1, one launch (start us, length us, event | category | flops | bytes accessed | tf_op | source)
XLA Modules:
  0.0 66.2 jit_solution(10408018240476180325)
XLA Ops:
  0.0 0.0 copy-start.2
  0.0 0.0 copy-start.3
  0.0 0.0 copy-start.1
  0.8 63.9 %step.1 = (bf16[2,64,4,128]{3,2,1,0:T(4,128)(2,1)S(1)}, f32[1,1]{1,0:T(1,128)}) custom-call(s32[1,1]{1,0:T(1,128)S(6)} %copy.70.cnt_ref, s32[3,1,512]{2,1,0:T(1,128)} %bitcast.132, bf16[512,128,128]{2,1,0:T(8,128)(2,1)} %bitcast.123, bf16[1024,4,128]{2,1,0:T(4,128)(2,1)} %bitcast.126, f32[2,64,4,128]{3,2,1,0:T(4,128)} %bitcast.127, ...), custom_call_target="tpu_custom_call" | custom-call | tf_op jit(solution)/shard_map/step/pallas_call | solution.py:484
  65.3 0.0 copy-done.2
  65.3 0.0 copy-done.3
  65.3 0.0 copy-done.1
  65.4 0.2 conditional.1
  65.6 0.7 copy.72
Async XLA Ops:
  0.0 65.3 %copy-start.2 = (f32[2,4,8192]{2,1,0:T(4,128)S(1)}, f32[2,4,8192]{2,1,0:T(4,128)}, u32[]{:S(2)}) copy-start(f32[2,4,8192]{2,1,0:T(4,128)} %param.24) | copy-start | bytes 786436
  0.0 65.3 %copy-start.3 = (s32[1,1,3,512]{3,1,2,0:T(1,128)S(1)}, s32[1,1,3,512]{3,1,2,0:T(1,128)}, u32[]{:S(2)}) copy-start(s32[1,1,3,512]{3,1,2,0:T(1,128)} %param.21) | copy-start | bytes 18436
  0.0 65.3 %copy-start.1 = (bf16[16,4,8192]{2,1,0:T(4,128)(2,1)S(1)}, bf16[16,4,8192]{2,1,0:T(4,128)(2,1)}, u32[]{:S(2)}) copy-start(bf16[16,4,8192]{2,1,0:T(4,128)(2,1)} %param.23) | copy-start | bytes 3145732

commit v6 on v5

--- a/solution.py
+++ b/solution.py
@@ -12,7 +12,7 @@
 CAP0 = 12
 CAPD = 64
 FAR = -(1 << 20)
-ORDER = (10, 11, 8, 9, 6, 14, 7, 15, 4, 12, 5, 13, 2, 3, 1)
+ORDER = (10, 11, 6, 14, 7, 15, 2, 3, 8, 9, 4, 12, 5, 13, 1)
 STAGED = (False, False)
 AT0 = 64
 
@@ -150,7 +150,7 @@
     order = ORDER if n_obs == len(ORDER) + 1 else range(1, n_obs)
     entered = greet(1, 1, n_src, n_obs)
     n_tiles = tiles_ref.shape[0]
-    chunk = min(32, n_tiles)
+    chunk = min(64, n_tiles)
     chunks = n_tiles // chunk
     width = tiles_ref.shape[2]
     coefs = hist_ref.shape[1]
@@ -316,9 +316,11 @@
         for c in range(coefs):
             drive[pl.ds(c * bd, bd), :] = total[:, c * width : (c + 1) * width]
 
+        some = min(32, bd)
+
         def pairs(turn):
-            for i in range(4):
-                b = turn * 8 + 2 * i
+            for i in range(some // 2):
+                b = turn * some + 2 * i
                 x0 = inc[which, b] - drive[pl.ds(b, coefs, stride=bd), :]
                 x1 = inc[which, b + 1] - drive[pl.ds(b + 1, coefs, stride=bd), :]
                 x = jnp.concatenate([x0, x1], axis=0).astype(jnp.bfloat16)
@@ -328,7 +330,7 @@
                 out_ref[which, b] = both[:coefs, :width].astype(jnp.bfloat16)
                 out_ref[which, b + 1] = both[coefs:, width:].astype(jnp.bfloat16)
 
-        each(bd // 8, pairs)
+        each(bd // some, pairs)
 
     take(tile, tile_sem)
     info_down.wait()
@@ -354,7 +356,8 @@
         gather(newest, send0.at[k], obs_peer(k, n_obs), CAP0, AT0, placed)
         send_new(k).start()
 
-    each(n_obs, gather_send_new, 1)
+    for k in order:
+        gather_send_new(k)
     gather(newest, rows0.at[pl.ds(me_o * CAP0, CAP0)], me_o, CAP0, AT0, placed)
     take_rows(send2, rows2, CAP, sem2)
     each(chunks, products(rows2))
@@ -365,13 +368,13 @@
     take_rows(send0, rows0, CAP0, sem0)
 
     def new_products(turn):
-        for i in range(0, 8, 2):
-            r = turn * 8 + i
+        for i in range(0, 32, 2):
+            r = turn * 32 + i
             two_products(
                 rows0[lst[1, r]], rows0[lst[1, r + 1]], tile[lst[0, r]], tile[lst[0, r + 1]], y_new, CAPD, r
             )
 
-    each(CAPD // 8, new_products)
+    each(CAPD // 32, new_products)
     value = jnp.concatenate([y_new[c * CAPD : (c + 1) * CAPD, :] for c in range(coefs)], axis=1)
     value = value.astype(jnp.bfloat16)
     for g in range(2):

time: 66.4 us -> 61.7 us (0.929)
  Pallas kernels: 63.9 us -> 59.2 us
    pallas_call x1, Pallas kernels: 63.9 us -> 59.2 us  [on_device(): pl.pallas_call(functools.partial(step_kernel, n_src, n_obs, bd), name='st...]
where the time goes in v6:
time: 61.7 us; the launch traced here: 61.5 us
  Pallas kernels  59.2 us (96%)
  between operations  1.43 us (2%)
  local copies, waits for them, and re-layouts  0.67 us (1%)
    pallas_call x1, Pallas kernels, on_device(): pl.pallas_call(functools.partial(step_kernel, n_src, n_obs, bd), name='st...  59.2 us

profile of v6, /device:TPU:1, one launch (start us, length us, event | category | flops | bytes accessed | tf_op | source)
XLA Modules:
  0.0 61.5 jit_solution(17695501531638064542)
XLA Ops:
  0.0 0.0 copy-start.2
  0.0 0.0 copy-start.3
  0.0 0.0 copy-start.1
  0.8 59.2 %step.1 = (bf16[2,64,4,128]{3,2,1,0:T(4,128)(2,1)S(1)}, f32[1,1]{1,0:T(1,128)}) custom-call(s32[1,1]{1,0:T(1,128)S(6)} %copy.70.cnt_ref, s32[3,1,512]{2,1,0:T(1,128)} %bitcast.132, bf16[512,128,128]{2,1,0:T(8,128)(2,1)} %bitcast.123, bf16[1024,4,128]{2,1,0:T(4,128)(2,1)} %bitcast.126, f32[2,64,4,128]{3,2,1,0:T(4,128)} %bitcast.127, ...), custom_call_target="tpu_custom_call" | custom-call | tf_op jit(solution)/shard_map/step/pallas_call | solution.py:487
  60.6 0.0 copy-done.2
  60.6 0.0 copy-done.3
  60.6 0.0 copy-done.1
  60.6 0.2 conditional.1
  60.9 0.7 %copy.72 = bf16[2,4,8192]{2,1,0:T(4,128)(2,1)} copy(bf16[2,4,8192]{2,1,0:T(4,128)(2,1)S(1)} %bitcast.130) | data formatting | bytes 262144
Async XLA Ops:
  0.0 60.6 %copy-start.2 = (f32[2,4,8192]{2,1,0:T(4,128)S(1)}, f32[2,4,8192]{2,1,0:T(4,128)}, u32[]{:S(2)}) copy-start(f32[2,4,8192]{2,1,0:T(4,128)} %param.24) | copy-start | bytes 786436
  0.0 60.6 %copy-start.3 = (s32[1,1,3,512]{3,1,2,0:T(1,128)S(1)}, s32[1,1,3,512]{3,1,2,0:T(1,128)}, u32[]{:S(2)}) copy-start(s32[1,1,3,512]{3,1,2,0:T(1,128)} %param.21) | copy-start | bytes 18436
  0.0 60.6 %copy-start.1 = (bf16[16,4,8192]{2,1,0:T(4,128)(2,1)S(1)}, bf16[16,4,8192]{2,1,0:T(4,128)(2,1)}, u32[]{:S(2)}) copy-start(bf16[16,4,8192]{2,1,0:T(4,128)(2,1)} %param.23) | copy-start | bytes 3145732

commit v7 on v6

--- a/solution.py
+++ b/solution.py
@@ -12,8 +12,8 @@
 CAP0 = 12
 CAPD = 64
 FAR = -(1 << 20)
-ORDER = (10, 11, 6, 14, 7, 15, 2, 3, 8, 9, 4, 12, 5, 13, 1)
-STAGED = (False, False)
+ORDER = (6, 14, 7, 15, 10, 11, 2, 3, 8, 9, 4, 12, 5, 13, 1)
+STAGED = (True, False)
 AT0 = 64
 
 
@@ -170,7 +170,8 @@
         return to_obs(k, n_obs, ask.at[obs_peer(k, n_obs)], asked.at[me_o], ask_sem.at[0], ask_sem.at[1])
 
     entered()
-    each(n_obs, lambda k: send_ask(k).start(), 1)
+    for k in order:
+        send_ask(k).start()
     build_list()
     info_down = pltpu.make_async_copy(info_v, info, load_sem.at[3])
     list_down = pltpu.make_async_copy(list_v, lst, load_sem.at[4])

time: 61.7 us -> 59 us (0.956)
  Pallas kernels: 59.2 us -> 56.6 us
    pallas_call x1, Pallas kernels: 59.2 us -> 56.6 us  [on_device(): pl.pallas_call(functools.partial(step_kernel, n_src, n_obs, bd), name='st...]
where the time goes in v7:
time: 59 us; the launch traced here: 58.9 us
  Pallas kernels  56.6 us (96%)
  between operations  1.43 us (2%)
  local copies, waits for them, and re-layouts  0.67 us (1%)
    pallas_call x1, Pallas kernels, on_device(): pl.pallas_call(functools.partial(step_kernel, n_src, n_obs, bd), name='st...  56.6 us

profile of v7, /device:TPU:1, one launch (start us, length us, event | category | flops | bytes accessed | tf_op | source)
XLA Modules:
  0.0 58.9 jit_solution(13106569244771326663)
XLA Ops:
  0.0 0.0 copy-start.2
  0.0 0.0 copy-start.3
  0.0 0.0 copy-start.1
  0.8 56.6 %step.1 = (bf16[2,64,4,128]{3,2,1,0:T(4,128)(2,1)S(1)}, f32[1,1]{1,0:T(1,128)}) custom-call(s32[1,1]{1,0:T(1,128)S(6)} %copy.70.cnt_ref, s32[3,1,512]{2,1,0:T(1,128)} %bitcast.132, bf16[512,128,128]{2,1,0:T(8,128)(2,1)} %bitcast.123, bf16[1024,4,128]{2,1,0:T(4,128)(2,1)} %bitcast.126, f32[2,64,4,128]{3,2,1,0:T(4,128)} %bitcast.127, ...), custom_call_target="tpu_custom_call" | custom-call | tf_op jit(solution)/shard_map/step/pallas_call | solution.py:488
  58.0 0.0 copy-done.2
  58.0 0.0 copy-done.3
  58.0 0.0 copy-done.1
  58.0 0.2 conditional.1
  58.3 0.7 %copy.72 = bf16[2,4,8192]{2,1,0:T(4,128)(2,1)} copy(bf16[2,4,8192]{2,1,0:T(4,128)(2,1)S(1)} %bitcast.130) | data formatting | bytes 262144
Async XLA Ops:
  0.0 58.0 %copy-start.2 = (f32[2,4,8192]{2,1,0:T(4,128)S(1)}, f32[2,4,8192]{2,1,0:T(4,128)}, u32[]{:S(2)}) copy-start(f32[2,4,8192]{2,1,0:T(4,128)} %param.24) | copy-start | bytes 786436
  0.0 58.0 %copy-start.3 = (s32[1,1,3,512]{3,1,2,0:T(1,128)S(1)}, s32[1,1,3,512]{3,1,2,0:T(1,128)}, u32[]{:S(2)}) copy-start(s32[1,1,3,512]{3,1,2,0:T(1,128)} %param.21) | copy-start | bytes 18436
  0.0 58.0 %copy-start.1 = (bf16[16,4,8192]{2,1,0:T(4,128)(2,1)S(1)}, bf16[16,4,8192]{2,1,0:T(4,128)(2,1)}, u32[]{:S(2)}) copy-start(bf16[16,4,8192]{2,1,0:T(4,128)(2,1)} %param.23) | copy-start | bytes 3145732

commit v8 on v7

--- a/solution.py
+++ b/solution.py
@@ -20,15 +20,13 @@
 def greet(src_peers, obs_peers, n_src, n_obs):
     me_s, me_o = lax.axis_index("src"), lax.axis_index("obs")
     barrier = pltpu.get_barrier_semaphore()
+    if obs_peers:
+        for k in ORDER if n_obs == len(ORDER) + 1 else range(1, n_obs):
+            pl.semaphore_signal(barrier, inc=1, device_id=(me_s, obs_peer(k, n_obs)), device_id_type=MESH)
     if src_peers:
         for k in range(1, n_src):
             pl.semaphore_signal(
                 barrier, inc=1, device_id=(lax.rem(me_s + k, n_src), me_o), device_id_type=MESH
-            )
-    if obs_peers:
-        for k in range(1, n_obs):
-            pl.semaphore_signal(
-                barrier, inc=1, device_id=(me_s, obs_peer(k, n_obs)), device_id_type=MESH
             )
     total = (n_src - 1) * src_peers + (n_obs - 1) * obs_peers
     return lambda: pl.semaphore_wait(barrier, total)
@@ -139,15 +137,19 @@
 
 
 def step_kernel(
-    n_src, n_obs, bd, cnt_ref, idx_ref, tiles_ref, hist_ref, inc_ref, near_ref,
+    n_src, n_obs, bd, cnt_hbm, idx_hbm, tiles_ref, hist_ref, inc_ref, near_ref,
     out_ref, crowded_ref,
-    ask, asked, info_v, list_v, req, info, lst, flags,
+    cnt_ref, idx_ref, ask, asked, info_v, list_v, req, info, lst, flags,
     tile, hist, inc, near, rows1, rows2, rows0, send1, send2, send0, mark,
     y_one, y_all, y_new, pick1, pick2, pick0, part_old, part1, part2, recv1, recv2, far_out, far_in, drive,
     tile_sem, load_sem, ask_sem, flag_sem, sem1, sem2, sem0, part_sem1, part_sem2, far_sem1, far_sem2,
 ):
     me_s, me_o = lax.axis_index("src"), lax.axis_index("obs")
     order = ORDER if n_obs == len(ORDER) + 1 else range(1, n_obs)
+    load_cnt = pltpu.make_async_copy(cnt_hbm, cnt_ref, load_sem.at[6])
+    load_idx = pltpu.make_async_copy(idx_hbm, idx_ref, load_sem.at[7])
+    load_cnt.start()
+    load_idx.start()
     entered = greet(1, 1, n_src, n_obs)
     n_tiles = tiles_ref.shape[0]
     chunk = min(64, n_tiles)
@@ -163,6 +165,8 @@
         return pltpu.make_async_copy(tiles_ref.at[at], tile.at[at], tile_sem)
 
     load_hist.start()
+    load_cnt.wait()
+    load_idx.wait()
     build_list = build_requests(n_src, n_obs, bd, hist_ref.shape[0], idx_ref, cnt_ref, ask, info_v, list_v)
     asked[me_o] = ask[me_o]
 
@@ -492,9 +496,10 @@
                 jax.ShapeDtypeStruct((2, bd, coefs, width), bf16),
                 jax.ShapeDtypeStruct((1, 1), f32),
             ),
-            in_specs=[vmem, vmem, hbm, hbm, hbm, hbm],
+            in_specs=[hbm] * 6,
             out_specs=(vmem, smem),
             scratch_shapes=[
+                pltpu.VMEM((1, 1), i32), pltpu.VMEM(index_rows.shape, i32),
                 pltpu.VMEM((n_obs, 1, 128), i32), pltpu.VMEM((n_obs, 1, 128), i32),
                 pltpu.VMEM((8, n_tiles), i32), pltpu.VMEM((8, 128), i32),
                 pltpu.SMEM((n_obs, 1, 128), i32), pltpu.SMEM((8, n_tiles), i32), pltpu.SMEM((8, 128), i32),
@@ -514,7 +519,7 @@
                 parts(f32), parts(bf16), parts(bf16), arrived, arrived,
                 pltpu.VMEM((bd, coefs * width), bf16), pltpu.VMEM((bd, coefs * width), bf16),
                 pltpu.VMEM((coefs * bd, width), f32),
-                dma, dma((6,)), dma((2,)), dma((2,)), dma((2,)), dma((2,)), dma((2,)), dma((3,)), dma((3,)), dma((2,)), dma((2,)),
+                dma, dma((8,)), dma((2,)), dma((2,)), dma((2,)), dma((2,)), dma((2,)), dma((3,)), dma((3,)), dma((2,)), dma((2,)),
             ],
             compiler_params=params(0),
         )(tile_count, index_rows, tile_rows, hist, drive, near_inverse)

time: 59 us -> 58.8 us (level)
  no operation moved by 1% of the time
where the time goes in v8:
time: 58.8 us; the launch traced here: 58.4 us
  Pallas kernels  56.1 us (95%)
  between operations  1.43 us (2%)
  local copies, waits for them, and re-layouts  0.67 us (1%)
    pallas_call x1, Pallas kernels, on_device(): pl.pallas_call(functools.partial(step_kernel, n_src, n_obs, bd), name='st...  56.1 us

profile of v8, /device:TPU:1, one launch (start us, length us, event | category | flops | bytes accessed | tf_op | source)
XLA Modules:
  0.0 58.4 jit_solution(11081181924658060321)
XLA Ops:
  0.0 0.0 copy-start.2
  0.0 0.0 copy-start.3
  0.0 0.0 copy-start.1
  0.8 56.1 %step.1 = (bf16[2,64,4,128]{3,2,1,0:T(4,128)(2,1)S(1)}, f32[1,1]{1,0:T(1,128)}) custom-call(s32[1,1]{1,0:T(1,128)S(6)} %copy.70.cnt_hbm, s32[3,1,512]{2,1,0:T(1,128)} %bitcast.132, bf16[512,128,128]{2,1,0:T(8,128)(2,1)} %bitcast.123, bf16[1024,4,128]{2,1,0:T(4,128)(2,1)} %bitcast.126, f32[2,64,4,128]{3,2,1,0:T(4,128)} %bitcast.127, ...), custom_call_target="tpu_custom_call" | custom-call | tf_op jit(solution)/shard_map/step/pallas_call | solution.py:492
  57.5 0.0 copy-done.2
  57.5 0.0 copy-done.3
  57.5 0.0 copy-done.1
  57.5 0.2 conditional.1
  57.7 0.7 %copy.72 = bf16[2,4,8192]{2,1,0:T(4,128)(2,1)} copy(bf16[2,4,8192]{2,1,0:T(4,128)(2,1)S(1)} %bitcast.130) | data formatting | bytes 262144
Async XLA Ops:
  0.0 57.5 %copy-start.2 = (f32[2,4,8192]{2,1,0:T(4,128)S(1)}, f32[2,4,8192]{2,1,0:T(4,128)}, u32[]{:S(2)}) copy-start(f32[2,4,8192]{2,1,0:T(4,128)} %param.24) | copy-start | bytes 786436
  0.0 57.5 %copy-start.3 = (s32[1,1,3,512]{3,1,2,0:T(1,128)S(1)}, s32[1,1,3,512]{3,1,2,0:T(1,128)}, u32[]{:S(2)}) copy-start(s32[1,1,3,512]{3,1,2,0:T(1,128)} %param.21) | copy-start | bytes 18436
  0.0 57.5 %copy-start.1 = (bf16[16,4,8192]{2,1,0:T(4,128)(2,1)S(1)}, bf16[16,4,8192]{2,1,0:T(4,128)(2,1)}, u32[]{:S(2)}) copy-start(bf16[16,4,8192]{2,1,0:T(4,128)(2,1)} %param.23) | copy-start | bytes 3145732

commit v9 on v7

--- a/solution.py
+++ b/solution.py
@@ -150,7 +150,7 @@
     order = ORDER if n_obs == len(ORDER) + 1 else range(1, n_obs)
     entered = greet(1, 1, n_src, n_obs)
     n_tiles = tiles_ref.shape[0]
-    chunk = min(64, n_tiles)
+    chunk = min(128, n_tiles)
     chunks = n_tiles // chunk
     width = tiles_ref.shape[2]
     coefs = hist_ref.shape[1]
@@ -317,7 +317,7 @@
         for c in range(coefs):
             drive[pl.ds(c * bd, bd), :] = total[:, c * width : (c + 1) * width]
 
-        some = min(32, bd)
+        some = min(64, bd)
 
         def pairs(turn):
             for i in range(some // 2):
@@ -369,13 +369,13 @@
     take_rows(send0, rows0, CAP0, sem0)
 
     def new_products(turn):
-        for i in range(0, 32, 2):
-            r = turn * 32 + i
+        for i in range(0, 64, 2):
+            r = turn * 64 + i
             two_products(
                 rows0[lst[1, r]], rows0[lst[1, r + 1]], tile[lst[0, r]], tile[lst[0, r + 1]], y_new, CAPD, r
             )
 
-    each(CAPD // 32, new_products)
+    each(CAPD // 64, new_products)
     value = jnp.concatenate([y_new[c * CAPD : (c + 1) * CAPD, :] for c in range(coefs)], axis=1)
     value = value.astype(jnp.bfloat16)
     for g in range(2):

time: 59 us -> 58 us (0.983)
  Pallas kernels: 56.6 us -> 55.5 us
    pallas_call x1, Pallas kernels: 56.6 us -> 55.5 us  [on_device(): pl.pallas_call(functools.partial(step_kernel, n_src, n_obs, bd), name='st...]
where the time goes in v9:
time: 58 us; the launch traced here: 57.8 us
  Pallas kernels  55.5 us (96%)
  between operations  1.43 us (2%)
  local copies, waits for them, and re-layouts  0.67 us (1%)
    pallas_call x1, Pallas kernels, on_device(): pl.pallas_call(functools.partial(step_kernel, n_src, n_obs, bd), name='st...  55.5 us

profile of v9, /device:TPU:1, one launch (start us, length us, event | category | flops | bytes accessed | tf_op | source)
XLA Modules:
  0.0 57.8 jit_solution(10472296501545746040)
XLA Ops:
  0.0 0.0 copy-start.2
  0.0 0.0 copy-start.3
  0.0 0.0 copy-start.1
  0.8 55.5 %step.1 = (bf16[2,64,4,128]{3,2,1,0:T(4,128)(2,1)S(1)}, f32[1,1]{1,0:T(1,128)}) custom-call(s32[1,1]{1,0:T(1,128)S(6)} %copy.70.cnt_ref, s32[3,1,512]{2,1,0:T(1,128)} %bitcast.132, bf16[512,128,128]{2,1,0:T(8,128)(2,1)} %bitcast.123, bf16[1024,4,128]{2,1,0:T(4,128)(2,1)} %bitcast.126, f32[2,64,4,128]{3,2,1,0:T(4,128)} %bitcast.127, ...), custom_call_target="tpu_custom_call" | custom-call | tf_op jit(solution)/shard_map/step/pallas_call | solution.py:488
  56.9 0.0 copy-done.2
  56.9 0.0 copy-done.3
  56.9 0.0 copy-done.1
  56.9 0.2 conditional.1
  57.2 0.7 %copy.72 = bf16[2,4,8192]{2,1,0:T(4,128)(2,1)} copy(bf16[2,4,8192]{2,1,0:T(4,128)(2,1)S(1)} %bitcast.130) | data formatting | bytes 262144
Async XLA Ops:
  0.0 56.9 %copy-start.2 = (f32[2,4,8192]{2,1,0:T(4,128)S(1)}, f32[2,4,8192]{2,1,0:T(4,128)}, u32[]{:S(2)}) copy-start(f32[2,4,8192]{2,1,0:T(4,128)} %param.24) | copy-start | bytes 786436
  0.0 56.9 %copy-start.3 = (s32[1,1,3,512]{3,1,2,0:T(1,128)S(1)}, s32[1,1,3,512]{3,1,2,0:T(1,128)}, u32[]{:S(2)}) copy-start(s32[1,1,3,512]{3,1,2,0:T(1,128)} %param.21) | copy-start | bytes 18436
  0.0 56.9 %copy-start.1 = (bf16[16,4,8192]{2,1,0:T(4,128)(2,1)S(1)}, bf16[16,4,8192]{2,1,0:T(4,128)(2,1)}, u32[]{:S(2)}) copy-start(bf16[16,4,8192]{2,1,0:T(4,128)(2,1)} %param.23) | copy-start | bytes 3145732
